TPU v7x, 32 devices: a whole 2x2x4 slice. The times are simulated.
32 devices in a mesh: groups: 2 (over y), expert: 4 (over z), dp: 4 (over x, core).
Axes of the slice: x: 2, y: 2, z: 4, core: 2. Of those that a mesh axis runs over, the one named last changes fastest.
Arguments:
- tokens: bfloat16 [2048, 1024], P(('groups', 'expert', 'dp')), parts along dimension 0, may hold values from -6 to 6
- expert_ids: int32 [2048, 8], P(('groups', 'expert', 'dp')), parts along dimension 0, may hold values from 0 to 31, all different within a row; in each aligned block of 64 rows (0 to 63, 64 to 127, ...) at most 32 rows name the same one
- route_scores: float32 [2048, 8], P(('groups', 'expert', 'dp')), parts along dimension 0, may hold values from 0.05 to 1
- w_gate: bfloat16 [32, 1024, 768], P('expert'), may hold values from -0.1875 to 0.1875
- w_up: bfloat16 [32, 1024, 768], P('expert'), may hold values from -0.1875 to 0.1875
- w_down: bfloat16 [32, 768, 1024], P('expert'), may hold values from -0.21875 to 0.21875
Outputs:
- mixed: bfloat16 [2048, 1024], P(('groups', 'expert', 'dp')), parts along dimension 0
There are 2 independent parts, one for each index of `groups`. A program takes and returns all parts, laid end to end along the dimension named above; an argument that names none is the same for every part. Nothing has to cross between parts.
Inputs may be any that keep to these rules, and one draw needn't show every extreme that they name: `expert_ids`: within the 64 rows of one device no expert is named by more than 32 rows, and in every draw some expert is named by exactly 32 rows of some device.
All inputs are finite; a program needn't handle non-finite values.
Results may differ from a plain program's by a relative error of at most 0.0064.
Values may be sent and summed in bfloat16 or wider, within the bound.
No kernel may reach another device: no remote copies, remote signals or barrier semaphores. Data moves between devices by JAX's collectives and lax.ppermute only.
A program may use at most 128 MiB of HBM per device.

v0:
```python
import functools

import jax
import jax.numpy as jnp
from jax import lax
from jax.experimental import pallas as pl
from jax.experimental.pallas import tpu as pltpu
from jax.sharding import PartitionSpec as P


SUBLANES, LANES = 8, 128
CHUNK = 256
GROUP = 4
MIB = 1 << 20
VMEM = pl.BlockSpec(memory_space=pltpu.VMEM)
ANY = pl.BlockSpec(memory_space=pl.ANY)


def slots_of(experts):
    return -(-experts // SUBLANES) * SUBLANES


def in_hbm(array):
    return pltpu.with_memory_space_constraint(array, pltpu.HBM)


def hidden_of(rows, gate_matrix, up_matrix):
    gate = jnp.dot(rows, gate_matrix, preferred_element_type=jnp.float32)
    up = jnp.dot(rows, up_matrix, preferred_element_type=jnp.float32)
    return (gate / (1.0 + jnp.exp(-gate)) * up).astype(jnp.bfloat16)


def tiles_of(array):
    rows, width = array.shape
    split = array.reshape(rows // SUBLANES, SUBLANES, width // LANES, LANES)
    return split.transpose(0, 2, 1, 3).reshape(-1, SUBLANES, LANES)


def pack_kernel(tile_hbm, id_hbm, score_hbm, out_ref, id_ref, score_ref, sems):
    tiles = tile_hbm.shape[0]
    copies = [
        pltpu.make_async_copy(id_hbm, id_ref, sems.at[0]),
        pltpu.make_async_copy(score_hbm, score_ref, sems.at[1]),
        pltpu.make_async_copy(tile_hbm, out_ref.at[pl.ds(0, tiles)], sems.at[2]),
    ]
    for copy in copies:
        copy.start()
    out_ref[tiles] = jnp.zeros((SUBLANES, LANES), jnp.bfloat16)
    out_ref[tiles + 1] = jnp.zeros((SUBLANES, LANES), jnp.bfloat16)
    top, count = id_ref.shape
    copies[0].wait()
    copies[1].wait()
    scores = score_ref[...]
    shares = scores / jnp.sum(scores, axis=0, keepdims=True)
    out_ref[tiles, :top, :count] = id_ref[...].astype(jnp.float32).astype(jnp.bfloat16)
    out_ref[tiles + 1, :top, :count] = shares.astype(jnp.bfloat16)
    copies[2].wait()


def pack(tokens, expert_ids, route_scores):
    tiles = tiles_of(tokens)
    count, top = expert_ids.shape
    return pl.pallas_call(
        pack_kernel,
        out_shape=pltpu.VMEM((tiles.shape[0] + 2, SUBLANES, LANES), jnp.bfloat16),
        in_specs=[ANY] * 3,
        out_specs=VMEM,
        scratch_shapes=[
            pltpu.VMEM((top, count), jnp.int32),
            pltpu.VMEM((top, count), jnp.float32),
            pltpu.SemaphoreType.DMA((3,)),
        ],
        compiler_params=pltpu.CompilerParams(vmem_limit_bytes=4 * MIB),
    )(in_hbm(tiles), in_hbm(expert_ids.T), in_hbm(route_scores.T))


def own_kernel(token_hbm, gate_hbm, up_hbm, gate_ref, up_ref, hidden_ref, rows_ref, sems):
    local_experts = gate_ref.shape[0]
    tokens = pltpu.make_async_copy(token_hbm, rows_ref, sems.at[2, 0])
    tokens.start()

    def load(member, which):
        source, target = ((gate_hbm, gate_ref), (up_hbm, up_ref))[which]
        return pltpu.make_async_copy(
            source.at[member], target.at[member], sems.at[which, member]
        )

    for member in range(local_experts):
        load(member, 0).start()
        load(member, 1).start()
    tokens.wait()

    def one_expert(member, carry):
        load(member, 0).wait()
        load(member, 1).wait()
        hidden_ref[member] = hidden_of(rows_ref[...], gate_ref[member], up_ref[member])
        return carry

    lax.fori_loop(0, local_experts, one_expert, 0)


def own_hidden(tokens, w_gate, w_up):
    local_experts, _, units = w_gate.shape
    count = tokens.shape[0]
    return pl.pallas_call(
        own_kernel,
        out_shape=[
            pltpu.VMEM(w_gate.shape, w_gate.dtype),
            pltpu.VMEM(w_up.shape, w_up.dtype),
            pltpu.VMEM((local_experts, count, units), jnp.bfloat16),
        ],
        in_specs=[ANY] * 3,
        out_specs=[VMEM] * 3,
        scratch_shapes=[
            pltpu.VMEM(tokens.shape, tokens.dtype),
            pltpu.SemaphoreType.DMA((3, local_experts)),
        ],
        compiler_params=pltpu.CompilerParams(vmem_limit_bytes=8 * MIB),
        cost_estimate=pl.CostEstimate(
            flops=4 * count * w_gate.size, bytes_accessed=4 * w_gate.size, transcendentals=0
        ),
    )(in_hbm(tokens), in_hbm(w_gate), in_hbm(w_up))


def spread_shares(packed_refs, spread_ref, count, top, held):
    first = lax.axis_index("expert") * held
    slots = spread_ref.shape[1]
    expert = lax.broadcasted_iota(jnp.int32, (slots, count), 0) + first
    for index, packed_ref in enumerate(packed_refs):
        tiles = packed_ref.shape[0] - 2
        ids = packed_ref[tiles].astype(jnp.float32).astype(jnp.int32)
        shares = packed_ref[tiles + 1].astype(jnp.float32)
        spread = jnp.zeros((slots, count), jnp.float32)
        for slot in range(top):
            named = expert == ids[slot : slot + 1, :count]
            spread += jnp.where(named, shares[slot : slot + 1, :count], 0.0)
        spread_ref[index * count : (index + 1) * count, :] = spread.T


def project_into(out_refs, total_ref, spread_ref, down_ref, hidden_at, count):
    local_experts, _, width = down_ref.shape
    for member in range(local_experts):
        weight = spread_ref[:, member : member + 1]
        for start in range(0, width, CHUNK):
            span = slice(start, min(start + CHUNK, width))
            scaled = weight * jnp.dot(
                hidden_at(member), down_ref[member, :, span], preferred_element_type=jnp.float32
            )
            if member:
                scaled = total_ref[:, span] + scaled
            if member < local_experts - 1:
                total_ref[:, span] = scaled
                continue
            for index, out_ref in enumerate(out_refs):
                part = scaled[index * count : (index + 1) * count]
                out_ref[:, span] = part.astype(out_ref.dtype)


def far_kernel(blocks, sent, top, *refs):
    packed_refs = refs[:blocks]
    gate_ref, up_ref, down_hbm = refs[blocks : blocks + 3]
    outs = refs[blocks + 3 :]
    out_refs, down_ref, near_ref = outs[:sent], outs[sent], outs[sent + 1]
    rows_ref, spread_ref, hidden_ref, total_ref, sems = outs[sent + 2 :]
    local_experts, width, units = gate_ref.shape
    count = rows_ref.shape[0] // blocks
    across = width // LANES
    tiles = packed_refs[0].shape[0] - 2
    loads = [
        pltpu.make_async_copy(down_hbm.at[member], down_ref.at[member], sems.at[member])
        for member in range(local_experts)
    ]
    for load in loads:
        load.start()
    for index in range(blocks):
        for tile in range(tiles):
            row = index * count + tile // across * SUBLANES
            column = tile % across * LANES
            rows_ref[row : row + SUBLANES, column : column + LANES] = packed_refs[index][tile]
    spread_shares(packed_refs[:sent], spread_ref, count, top, local_experts)
    for member in range(local_experts):
        for start in range(0, units, CHUNK):
            span = slice(start, min(start + CHUNK, units))
            hidden = hidden_of(rows_ref[...], gate_ref[member, :, span], up_ref[member, :, span])
            hidden_ref[member, :, span] = hidden[: sent * count]
            if sent < blocks:
                near_ref[member, :, span] = hidden[sent * count :]
    for load in loads:
        load.wait()
    project_into(
        out_refs, total_ref, spread_ref, down_ref, lambda member: hidden_ref[member], count
    )


def far(packed, sent, gate, up, w_down, count, top):
    blocks = len(packed)
    local_experts, units, width = w_down.shape
    rows = blocks * count
    near_rows = max(rows - sent * count, SUBLANES)
    *parts, down, near_hidden = pl.pallas_call(
        functools.partial(far_kernel, blocks, sent, top),
        out_shape=[jax.ShapeDtypeStruct((count, width), jnp.bfloat16)] * sent
        + [
            pltpu.VMEM(w_down.shape, w_down.dtype),
            pltpu.VMEM((local_experts, near_rows, units), jnp.bfloat16),
        ],
        in_specs=[VMEM] * (blocks + 2) + [ANY],
        out_specs=[VMEM] * (sent + 2),
        scratch_shapes=[
            pltpu.VMEM((rows, width), jnp.bfloat16),
            pltpu.VMEM((sent * count, slots_of(local_experts)), jnp.float32),
            pltpu.VMEM((local_experts, sent * count, units), jnp.bfloat16),
            pltpu.VMEM((sent * count, width), jnp.float32),
            pltpu.SemaphoreType.DMA((local_experts,)),
        ],
        compiler_params=pltpu.CompilerParams(vmem_limit_bytes=12 * MIB),
        cost_estimate=pl.CostEstimate(
            flops=6 * rows * w_down.size, bytes_accessed=2 * w_down.size, transcendentals=0
        ),
    )(*packed, gate, up, in_hbm(w_down))
    return parts, down, near_hidden


def near_kernel(top, *refs):
    packed_refs, hidden_refs, down_ref = refs[:2], refs[2:4], refs[4]
    out_refs = refs[5:7]
    spread_ref, hidden_ref, total_ref = refs[7:]
    count = hidden_refs[0].shape[1]
    spread_shares(packed_refs, spread_ref, count, top, down_ref.shape[0])
    hidden_ref[:, :count, :] = hidden_refs[0][...]
    hidden_ref[:, count:, :] = hidden_refs[1][...]
    project_into(
        out_refs, total_ref, spread_ref, down_ref, lambda member: hidden_ref[member], count
    )


def near(packed, hiddens, down, top):
    local_experts, count, units = hiddens[0].shape
    width = down.shape[2]
    return pl.pallas_call(
        functools.partial(near_kernel, top),
        out_shape=[
            jax.ShapeDtypeStruct((count, width), jnp.float32),
            jax.ShapeDtypeStruct((count, width), jnp.bfloat16),
        ],
        in_specs=[VMEM] * 5,
        out_specs=[VMEM] * 2,
        scratch_shapes=[
            pltpu.VMEM((2 * count, slots_of(local_experts)), jnp.float32),
            pltpu.VMEM((local_experts, 2 * count, units), jnp.bfloat16),
            pltpu.VMEM((2 * count, width), jnp.float32),
        ],
        compiler_params=pltpu.CompilerParams(vmem_limit_bytes=8 * MIB),
        cost_estimate=pl.CostEstimate(
            flops=4 * count * down.size, bytes_accessed=2 * down.size, transcendentals=0
        ),
    )(*packed, *hiddens, down)


def exchange(array, pairs):
    return lax.ppermute(array, "expert", pairs)


def per_device(tokens, expert_ids, route_scores, w_gate, w_up, w_down):
    peers = lax.axis_size("expert")
    count, top = expert_ids.shape
    packed = pack(tokens, expert_ids, route_scores)
    if peers == 4:
        pairs = {shift: [(i, i ^ shift) for i in range(peers)] for shift in (2, 3, 1)}
        got = {s: exchange(packed, pairs[s]) for s in pairs}
        gate, up, own = own_hidden(tokens, w_gate, w_up)
        parts, down, beside = far([got[2], got[3], got[1]], 2, gate, up, w_down, count, top)
        back = [exchange(part, pairs[s]) for part, s in zip(parts, (2, 3))]
        total, part = near([packed, got[1]], [own, beside], down, top)
        back.append(exchange(part, pairs[1]))
        for part in back:
            total = total + part.astype(jnp.float32)
        return total.astype(jnp.bfloat16)
    got = lax.all_gather(packed, "expert")
    gate, up, _ = own_hidden(tokens, w_gate, w_up)
    parts = []
    for start in range(0, peers, GROUP):
        here = [got[i] for i in range(start, min(start + GROUP, peers))]
        parts += far(here, len(here), gate, up, w_down, count, top)[0]
    back = lax.all_to_all(jnp.stack(parts), "expert", 0, 0, tiled=True)
    return jnp.sum(back.astype(jnp.float32), axis=0).astype(jnp.bfloat16)


def solution(mesh):
    split = P(("groups", "expert", "dp"), None)
    held = P("expert", None, None)
    return jax.shard_map(
        per_device,
        mesh=mesh,
        in_specs=(split, split, split, held, held, held),
        out_specs=split,
        check_vma=False,
    )
```

profile of v0, /device:TPU:0, one launch (start us, length us, event | category | flops | bytes accessed | tf_op | source)
XLA Modules:
  0.0 44.5 jit_solution(3171016725952796047)
XLA Ops:
  0.0 1.0 %shard_map.64.refs_0_ = bf16[66,8,128]{2,1,0:T(8,128)(2,1)S(1)} custom-call(bf16[64,8,128]{2,1,0:T(8,128)(2,1)} %bitcast.7, s32[8,64]{1,0:T(8,128)} %bitcast.8, f32[8,64]{1,0:T(8,128)} %bitcast.9), custom_call_target="tpu_custom_call" | custom-call | tf_op jit(solution)/shard_map/pallas_call | solution.py:63
  1.0 5.1 %collective-permute-start.2 = (bf16[66,8,128]{2,1,0:T(8,128)(2,1)S(1)}, bf16[66,8,128]{2,1,0:T(8,128)(2,1)S(1)}, u32[]{:S(2)}, u32[]{:S(2)}) collective-permute-start(bf16[66,8,128]{2,1,0:T(8,128)(2,1)S(1)} %shard_map.64.refs_0_), channel_id=1, source_target_pairs={{0,12},{4,8},{8,4},{12,0},{1,13},{5,9},{9,5},{13,1},{2,14},{6,10},... | collective-permute-start | bytes 405512 | tf_op jit(solution)/shard_map/ppermute | solution.py:261
  6.1 0.0 collective-permute-start.1
  6.1 0.6 %collective-permute-start = (bf16[66,8,128]{2,1,0:T(8,128)(2,1)S(1)}, bf16[66,8,128]{2,1,0:T(8,128)(2,1)S(1)}, u32[]{:S(2)}, u32[]{:S(2)}) collective-permute-start(bf16[66,8,128]{2,1,0:T(8,128)(2,1)S(1)} %shard_map.64.refs_0_), channel_id=1, source_target_pairs={{0,4},{4,0},{8,12},{12,8},{1,5},{5,1},{9,13},{13,9},{2,6},{6,2},{1... | collective-permute-start | bytes 405512 | tf_op jit(solution)/shard_map/ppermute | solution.py:261
  6.8 9.2 %shard_map.65 = (bf16[8,1024,768]{2,1,0:T(8,128)(2,1)S(1)}, bf16[8,1024,768]{2,1,0:T(8,128)(2,1)S(1)}, bf16[8,64,768]{2,1,0:T(8,128)(2,1)S(1)}) custom-call(bf16[64,1024]{1,0:T(8,128)(2,1)} %token_hbm.1, bf16[8,1024,768]{2,1,0:T(8,128)(2,1)} %gate_hbm.1, bf16[8,1024,768]{2,1,0:T(8,128)(2,1)} %up_hbm.1), custom_call_target="tpu_custom_call" | custom-call | flops 1610612736 | bytes 25165824 | tf_op jit(solution)/shard_map/pallas_call | solution.py:105
  15.9 0.0 collective-permute-done.2.refs_1_
  15.9 1.6 %collective-permute-done.1.refs_0_ = bf16[66,8,128]{2,1,0:T(8,128)(2,1)S(1)} collective-permute-done((bf16[66,8,128]{2,1,0:T(8,128)(2,1)S(1)}, bf16[66,8,128]{2,1,0:T(8,128)(2,1)S(1)}, u32[]{:S(2)}, u32[]{:S(2)}) %collective-permute-start.1) | collective-permute-done | bytes 135200 | tf_op jit(solution)/shard_map/ppermute | solution.py:261
  17.5 0.0 collective-permute-done.refs_2_.refs_1_
  17.5 11.6 %shard_map.66 = (bf16[64,1024]{1,0:T(8,128)(2,1)S(1)}, bf16[64,1024]{1,0:T(8,128)(2,1)S(1)}, bf16[8,768,1024]{2,1,0:T(8,128)(2,1)S(1)}, bf16[8,64,768]{2,1,0:T(8,128)(2,1)S(1)}) custom-call(bf16[66,8,128]{2,1,0:T(8,128)(2,1)S(1)} %collective-permute-done.1.refs_0_, bf16[66,8,128]{2,1,0:T(8,128)(2,1)S(1)} %collective-permute-done.2.refs_1_, ...), custom_call_target="tpu_custom_call" | custom-call | flops 7247757312 | bytes 12582912 | tf_op jit(solution)/shard_map/pallas_call | solution.py:200
  29.1 2.0 %shard_map.67 = (f32[64,1024]{1,0:T(8,128)S(1)}, bf16[64,1024]{1,0:T(8,128)(2,1)S(1)}) custom-call(bf16[66,8,128]{2,1,0:T(8,128)(2,1)S(1)} %shard_map.64.refs_0_, bf16[66,8,128]{2,1,0:T(8,128)(2,1)S(1)} %collective-permute-done.refs_2_.refs_1_, bf16[8,64,768]{2,1,0:T(8,128)(2,1)S(1)} %get-tuple-element.14.refs_2_, ...), custom_call_target="tpu_custom_call" | custom-call | flops 1610612736 | bytes 12582912 | tf_op jit(solution)/shard_map/pallas_call | solution.py:240
  31.2 0.1 collective-permute-start.5
  31.2 3.0 %collective-permute-start.3 = (bf16[64,1024]{1,0:T(8,128)(2,1)S(1)}, bf16[64,1024]{1,0:T(8,128)(2,1)S(1)}, u32[]{:S(2)}, u32[]{:S(2)}) collective-permute-start(bf16[64,1024]{1,0:T(8,128)(2,1)S(1)} %get-tuple-element.20), channel_id=1, source_target_pairs={{0,8},{4,12},{8,0},{12,4},{1,9},{5,13},{9,1},{13,5},{2,10},{6,14},... | collective-permute-start | bytes 393224 | tf_op jit(solution)/shard_map/ppermute | solution.py:261
  34.3 1.3 %collective-permute-start.4 = (bf16[64,1024]{1,0:T(8,128)(2,1)S(1)}, bf16[64,1024]{1,0:T(8,128)(2,1)S(1)}, u32[]{:S(2)}, u32[]{:S(2)}) collective-permute-start(bf16[64,1024]{1,0:T(8,128)(2,1)S(1)} %get-tuple-element.21), channel_id=1, source_target_pairs={{0,12},{4,8},{8,4},{12,0},{1,13},{5,9},{9,5},{13,1},{2,14},{6,10},... | collective-permute-start | bytes 393224 | tf_op jit(solution)/shard_map/ppermute | solution.py:261
  35.6 2.0 %collective-permute-done.5 = bf16[64,1024]{1,0:T(8,128)(2,1)S(1)} collective-permute-done((bf16[64,1024]{1,0:T(8,128)(2,1)S(1)}, bf16[64,1024]{1,0:T(8,128)(2,1)S(1)}, u32[]{:S(2)}, u32[]{:S(2)}) %collective-permute-start.5) | collective-permute-done | bytes 131104 | tf_op jit(solution)/shard_map/ppermute | solution.py:261
  37.7 6.1 %collective-permute-done.3 = bf16[64,1024]{1,0:T(8,128)(2,1)S(1)} collective-permute-done((bf16[64,1024]{1,0:T(8,128)(2,1)S(1)}, bf16[64,1024]{1,0:T(8,128)(2,1)S(1)}, u32[]{:S(2)}, u32[]{:S(2)}) %collective-permute-start.3) | collective-permute-done | bytes 131104 | tf_op jit(solution)/shard_map/ppermute | solution.py:261
  43.8 0.0 collective-permute-done.4
  43.8 0.7 %add_convert_fusion = bf16[64,1024]{1,0:T(8,128)(2,1)} fusion(bf16[64,1024]{1,0:T(8,128)(2,1)S(1)} %collective-permute-done.5, bf16[64,1024]{1,0:T(8,128)(2,1)S(1)} %collective-permute-done.4, f32[64,1024]{1,0:T(8,128)S(1)} %get-tuple-element.19, bf16[64,1024]{1,0:T(8,128)(2,1)S(1)} %collective-permute-done.3), kind=kLoop, calls=%fused_computation | loop fusion | flops 458752 | bytes 786432 | tf_op jit(solution)/shard_map/convert_element_type | solution.py:278
Async XLA Ops:
  1.0 15.0 %collective-permute-start.2 = (bf16[66,8,128]{2,1,0:T(8,128)(2,1)S(1)}, bf16[66,8,128]{2,1,0:T(8,128)(2,1)S(1)}, u32[]{:S(2)}, u32[]{:S(2)}) collective-permute-start(bf16[66,8,128]{2,1,0:T(8,128)(2,1)S(1)} %shard_map.64.refs_0_), channel_id=1, source_target_pairs={{0,12},{4,8},{8,4},{12,0},{1,13},{5,9},{9,5},{13,1},{2,14},{6,10},... | collective-permute-start | bytes 405512 | tf_op jit(solution)/shard_map/ppermute | solution.py:261
  6.1 11.4 %collective-permute-start.1 = (bf16[66,8,128]{2,1,0:T(8,128)(2,1)S(1)}, bf16[66,8,128]{2,1,0:T(8,128)(2,1)S(1)}, u32[]{:S(2)}, u32[]{:S(2)}) collective-permute-start(bf16[66,8,128]{2,1,0:T(8,128)(2,1)S(1)} %shard_map.64.refs_0_), channel_id=1, source_target_pairs={{0,8},{4,12},{8,0},{12,4},{1,9},{5,13},{9,1},{13,5},{2,10},{6,14},... | collective-permute-start | bytes 405512 | tf_op jit(solution)/shard_map/ppermute | solution.py:261
  6.1 11.4 %collective-permute-start = (bf16[66,8,128]{2,1,0:T(8,128)(2,1)S(1)}, bf16[66,8,128]{2,1,0:T(8,128)(2,1)S(1)}, u32[]{:S(2)}, u32[]{:S(2)}) collective-permute-start(bf16[66,8,128]{2,1,0:T(8,128)(2,1)S(1)} %shard_map.64.refs_0_), channel_id=1, source_target_pairs={{0,4},{4,0},{8,12},{12,8},{1,5},{5,1},{9,13},{13,9},{2,6},{6,2},{1... | collective-permute-start | bytes 405512 | tf_op jit(solution)/shard_map/ppermute | solution.py:261
  31.2 6.5 %collective-permute-start.5 = (bf16[64,1024]{1,0:T(8,128)(2,1)S(1)}, bf16[64,1024]{1,0:T(8,128)(2,1)S(1)}, u32[]{:S(2)}, u32[]{:S(2)}) collective-permute-start(bf16[64,1024]{1,0:T(8,128)(2,1)S(1)} %get-tuple-element.22), channel_id=1, source_target_pairs={{0,4},{4,0},{8,12},{12,8},{1,5},{5,1},{9,13},{13,9},{2,6},{6,2},{1... | collective-permute-start | bytes 393224 | tf_op jit(solution)/shard_map/ppermute | solution.py:261
  31.2 12.5 %collective-permute-start.3 = (bf16[64,1024]{1,0:T(8,128)(2,1)S(1)}, bf16[64,1024]{1,0:T(8,128)(2,1)S(1)}, u32[]{:S(2)}, u32[]{:S(2)}) collective-permute-start(bf16[64,1024]{1,0:T(8,128)(2,1)S(1)} %get-tuple-element.20), channel_id=1, source_target_pairs={{0,8},{4,12},{8,0},{12,4},{1,9},{5,13},{9,1},{13,5},{2,10},{6,14},... | collective-permute-start | bytes 393224 | tf_op jit(solution)/shard_map/ppermute | solution.py:261
  34.3 9.5 %collective-permute-start.4 = (bf16[64,1024]{1,0:T(8,128)(2,1)S(1)}, bf16[64,1024]{1,0:T(8,128)(2,1)S(1)}, u32[]{:S(2)}, u32[]{:S(2)}) collective-permute-start(bf16[64,1024]{1,0:T(8,128)(2,1)S(1)} %get-tuple-element.21), channel_id=1, source_target_pairs={{0,12},{4,8},{8,4},{12,0},{1,13},{5,9},{9,5},{13,1},{2,14},{6,10},... | collective-permute-start | bytes 393224 | tf_op jit(solution)/shard_map/ppermute | solution.py:261
where the time goes:
time: 44.7 us; the launch traced here: 44.5 us
  Pallas kernels  23.7 us (53%)
  starting transfers between devices  10.2 us (23%)
  waiting for transfers between devices  9.77 us (22%)
  other arithmetic  0.73 us (2%)
    pallas_call x1, Pallas kernels, far(): pl.pallas_call(functools.partial(far_kernel, blocks, sent, top), out_shap...  11.6 us
    ppermute x6, starting transfers between devices, exchange(): return lax.ppermute(array, 'expert', pairs)  10.2 us
    ppermute x6, waiting for transfers between devices, exchange(): return lax.ppermute(array, 'expert', pairs)  9.77 us
    pallas_call x1, Pallas kernels, own_hidden(): pl.pallas_call(own_kernel, out_shape=[pltpu.VMEM(w_gate.shape, w_gate.dty...  9.15 us
    pallas_call x1, Pallas kernels, near(): pl.pallas_call(functools.partial(near_kernel, top), out_shape=[jax.ShapeD...  2.02 us
    pallas_call x1, Pallas kernels, pack(): pl.pallas_call(pack_kernel, out_shape=pltpu.VMEM((tiles.shape[0] + 2, SUB...  0.96 us
  transfers between devices with their start and end apart: 6, of which 3 were waited for; matrix products, arithmetic and copies ran while one was open for 0% of the time, Pallas kernels for 21%

commit v1 on v0

--- a/solution.py
+++ b/solution.py
@@ -166,12 +166,14 @@
     count = rows_ref.shape[0] // blocks
     across = width // LANES
     tiles = packed_refs[0].shape[0] - 2
-    loads = [
-        pltpu.make_async_copy(down_hbm.at[member], down_ref.at[member], sems.at[member])
-        for member in range(local_experts)
-    ]
-    for load in loads:
-        load.start()
+
+    def load(member):
+        return pltpu.make_async_copy(down_hbm.at[member], down_ref.at[member], sems.at[member])
+
+    @pl.loop(0, local_experts)
+    def _(member):
+        load(member).start()
+
     for index in range(blocks):
         for tile in range(tiles):
             row = index * count + tile // across * SUBLANES
@@ -185,8 +187,8 @@
             hidden_ref[member, :, span] = hidden[: sent * count]
             if sent < blocks:
                 near_ref[member, :, span] = hidden[sent * count :]
-    for load in loads:
-        load.wait()
+    for member in range(local_experts):
+        load(member).wait()
     project_into(
         out_refs, total_ref, spread_ref, down_ref, lambda member: hidden_ref[member], count
     )

time: 44.7 us -> 40.7 us (0.911)
  Pallas kernels: 23.7 us -> 19.8 us
    pallas_call x1, Pallas kernels: 11.6 us -> 7.63 us  [far(): pl.pallas_call(functools.partial(far_kernel, blocks, sent, top), out_shap...]
  transfers between devices with their start and end apart: 6 -> 6, of which waited for: 3 -> 3; matrix products, arithmetic and copies ran while one was open for 0% -> 0% of each run, Pallas kernels for 21% -> 23%
where the time goes in v1:
time: 40.7 us; the launch traced here: 40.5 us
  Pallas kernels  19.8 us (49%)
  starting transfers between devices  10.2 us (25%)
  waiting for transfers between devices  9.77 us (24%)
  other arithmetic  0.73 us (2%)
    ppermute x6, starting transfers between devices, exchange(): return lax.ppermute(array, 'expert', pairs)  10.2 us
    ppermute x6, waiting for transfers between devices, exchange(): return lax.ppermute(array, 'expert', pairs)  9.77 us
    pallas_call x1, Pallas kernels, own_hidden(): pl.pallas_call(own_kernel, out_shape=[pltpu.VMEM(w_gate.shape, w_gate.dty...  9.15 us
    pallas_call x1, Pallas kernels, far(): pl.pallas_call(functools.partial(far_kernel, blocks, sent, top), out_shap...  7.63 us
    pallas_call x1, Pallas kernels, near(): pl.pallas_call(functools.partial(near_kernel, top), out_shape=[jax.ShapeD...  2.02 us
    pallas_call x1, Pallas kernels, pack(): pl.pallas_call(pack_kernel, out_shape=pltpu.VMEM((tiles.shape[0] + 2, SUB...  0.96 us
  transfers between devices with their start and end apart: 6, of which 3 were waited for; matrix products, arithmetic and copies ran while one was open for 0% of the time, Pallas kernels for 23%

profile of v1, /device:TPU:0, one launch (start us, length us, event | category | flops | bytes accessed | tf_op | source)
XLA Modules:
  0.0 40.5 jit_solution(13898562086291969739)
XLA Ops:
  0.0 1.0 %shard_map.64.refs_0_ = bf16[66,8,128]{2,1,0:T(8,128)(2,1)S(1)} custom-call(bf16[64,8,128]{2,1,0:T(8,128)(2,1)} %bitcast.7, s32[8,64]{1,0:T(8,128)} %bitcast.8, f32[8,64]{1,0:T(8,128)} %bitcast.9), custom_call_target="tpu_custom_call" | custom-call | tf_op jit(solution)/shard_map/pallas_call | solution.py:63
  1.0 5.1 %collective-permute-start.2 = (bf16[66,8,128]{2,1,0:T(8,128)(2,1)S(1)}, bf16[66,8,128]{2,1,0:T(8,128)(2,1)S(1)}, u32[]{:S(2)}, u32[]{:S(2)}) collective-permute-start(bf16[66,8,128]{2,1,0:T(8,128)(2,1)S(1)} %shard_map.64.refs_0_), channel_id=1, source_target_pairs={{0,12},{4,8},{8,4},{12,0},{1,13},{5,9},{9,5},{13,1},{2,14},{6,10},... | collective-permute-start | bytes 405512 | tf_op jit(solution)/shard_map/ppermute | solution.py:263
  6.1 0.0 collective-permute-start.1
  6.1 0.6 %collective-permute-start = (bf16[66,8,128]{2,1,0:T(8,128)(2,1)S(1)}, bf16[66,8,128]{2,1,0:T(8,128)(2,1)S(1)}, u32[]{:S(2)}, u32[]{:S(2)}) collective-permute-start(bf16[66,8,128]{2,1,0:T(8,128)(2,1)S(1)} %shard_map.64.refs_0_), channel_id=1, source_target_pairs={{0,4},{4,0},{8,12},{12,8},{1,5},{5,1},{9,13},{13,9},{2,6},{6,2},{1... | collective-permute-start | bytes 405512 | tf_op jit(solution)/shard_map/ppermute | solution.py:263
  6.8 9.2 %shard_map.65 = (bf16[8,1024,768]{2,1,0:T(8,128)(2,1)S(1)}, bf16[8,1024,768]{2,1,0:T(8,128)(2,1)S(1)}, bf16[8,64,768]{2,1,0:T(8,128)(2,1)S(1)}) custom-call(bf16[64,1024]{1,0:T(8,128)(2,1)} %token_hbm.1, bf16[8,1024,768]{2,1,0:T(8,128)(2,1)} %gate_hbm.1, bf16[8,1024,768]{2,1,0:T(8,128)(2,1)} %up_hbm.1), custom_call_target="tpu_custom_call" | custom-call | flops 1610612736 | bytes 25165824 | tf_op jit(solution)/shard_map/pallas_call | solution.py:105
  15.9 0.0 collective-permute-done.2.refs_1_
  15.9 1.6 %collective-permute-done.1.refs_0_ = bf16[66,8,128]{2,1,0:T(8,128)(2,1)S(1)} collective-permute-done((bf16[66,8,128]{2,1,0:T(8,128)(2,1)S(1)}, bf16[66,8,128]{2,1,0:T(8,128)(2,1)S(1)}, u32[]{:S(2)}, u32[]{:S(2)}) %collective-permute-start.1) | collective-permute-done | bytes 135200 | tf_op jit(solution)/shard_map/ppermute | solution.py:263
  17.5 0.0 collective-permute-done.refs_2_.refs_1_
  17.5 7.6 %shard_map.66 = (bf16[64,1024]{1,0:T(8,128)(2,1)S(1)}, bf16[64,1024]{1,0:T(8,128)(2,1)S(1)}, bf16[8,768,1024]{2,1,0:T(8,128)(2,1)S(1)}, bf16[8,64,768]{2,1,0:T(8,128)(2,1)S(1)}) custom-call(bf16[66,8,128]{2,1,0:T(8,128)(2,1)S(1)} %collective-permute-done.1.refs_0_, bf16[66,8,128]{2,1,0:T(8,128)(2,1)S(1)} %collective-permute-done.2.refs_1_, ...), custom_call_target="tpu_custom_call" | custom-call | flops 7247757312 | bytes 12582912 | tf_op jit(solution)/shard_map/pallas_call | solution.py:202
  25.2 2.0 %shard_map.67 = (f32[64,1024]{1,0:T(8,128)S(1)}, bf16[64,1024]{1,0:T(8,128)(2,1)S(1)}) custom-call(bf16[66,8,128]{2,1,0:T(8,128)(2,1)S(1)} %shard_map.64.refs_0_, bf16[66,8,128]{2,1,0:T(8,128)(2,1)S(1)} %collective-permute-done.refs_2_.refs_1_, bf16[8,64,768]{2,1,0:T(8,128)(2,1)S(1)} %get-tuple-element.14.refs_2_, ...), custom_call_target="tpu_custom_call" | custom-call | flops 1610612736 | bytes 12582912 | tf_op jit(solution)/shard_map/pallas_call | solution.py:242
  27.2 0.1 collective-permute-start.5
  27.3 3.1 %collective-permute-start.3 = (bf16[64,1024]{1,0:T(8,128)(2,1)S(1)}, bf16[64,1024]{1,0:T(8,128)(2,1)S(1)}, u32[]{:S(2)}, u32[]{:S(2)}) collective-permute-start(bf16[64,1024]{1,0:T(8,128)(2,1)S(1)} %get-tuple-element.20), channel_id=1, source_target_pairs={{0,8},{4,12},{8,0},{12,4},{1,9},{5,13},{9,1},{13,5},{2,10},{6,14},... | collective-permute-start | bytes 393224 | tf_op jit(solution)/shard_map/ppermute | solution.py:263
  30.3 1.3 %collective-permute-start.4 = (bf16[64,1024]{1,0:T(8,128)(2,1)S(1)}, bf16[64,1024]{1,0:T(8,128)(2,1)S(1)}, u32[]{:S(2)}, u32[]{:S(2)}) collective-permute-start(bf16[64,1024]{1,0:T(8,128)(2,1)S(1)} %get-tuple-element.21), channel_id=1, source_target_pairs={{0,12},{4,8},{8,4},{12,0},{1,13},{5,9},{9,5},{13,1},{2,14},{6,10},... | collective-permute-start | bytes 393224 | tf_op jit(solution)/shard_map/ppermute | solution.py:263
  31.7 2.0 %collective-permute-done.5 = bf16[64,1024]{1,0:T(8,128)(2,1)S(1)} collective-permute-done((bf16[64,1024]{1,0:T(8,128)(2,1)S(1)}, bf16[64,1024]{1,0:T(8,128)(2,1)S(1)}, u32[]{:S(2)}, u32[]{:S(2)}) %collective-permute-start.5) | collective-permute-done | bytes 131104 | tf_op jit(solution)/shard_map/ppermute | solution.py:263
  33.7 6.1 %collective-permute-done.3 = bf16[64,1024]{1,0:T(8,128)(2,1)S(1)} collective-permute-done((bf16[64,1024]{1,0:T(8,128)(2,1)S(1)}, bf16[64,1024]{1,0:T(8,128)(2,1)S(1)}, u32[]{:S(2)}, u32[]{:S(2)}) %collective-permute-start.3) | collective-permute-done | bytes 131104 | tf_op jit(solution)/shard_map/ppermute | solution.py:263
  39.8 0.0 collective-permute-done.4
  39.8 0.7 %add_convert_fusion = bf16[64,1024]{1,0:T(8,128)(2,1)} fusion(bf16[64,1024]{1,0:T(8,128)(2,1)S(1)} %collective-permute-done.5, bf16[64,1024]{1,0:T(8,128)(2,1)S(1)} %collective-permute-done.4, f32[64,1024]{1,0:T(8,128)S(1)} %get-tuple-element.19, bf16[64,1024]{1,0:T(8,128)(2,1)S(1)} %collective-permute-done.3), kind=kLoop, calls=%fused_computation | loop fusion | flops 458752 | bytes 786432 | tf_op jit(solution)/shard_map/convert_element_type | solution.py:280
Async XLA Ops:
  1.0 15.0 %collective-permute-start.2 = (bf16[66,8,128]{2,1,0:T(8,128)(2,1)S(1)}, bf16[66,8,128]{2,1,0:T(8,128)(2,1)S(1)}, u32[]{:S(2)}, u32[]{:S(2)}) collective-permute-start(bf16[66,8,128]{2,1,0:T(8,128)(2,1)S(1)} %shard_map.64.refs_0_), channel_id=1, source_target_pairs={{0,12},{4,8},{8,4},{12,0},{1,13},{5,9},{9,5},{13,1},{2,14},{6,10},... | collective-permute-start | bytes 405512 | tf_op jit(solution)/shard_map/ppermute | solution.py:263
  6.1 11.4 %collective-permute-start.1 = (bf16[66,8,128]{2,1,0:T(8,128)(2,1)S(1)}, bf16[66,8,128]{2,1,0:T(8,128)(2,1)S(1)}, u32[]{:S(2)}, u32[]{:S(2)}) collective-permute-start(bf16[66,8,128]{2,1,0:T(8,128)(2,1)S(1)} %shard_map.64.refs_0_), channel_id=1, source_target_pairs={{0,8},{4,12},{8,0},{12,4},{1,9},{5,13},{9,1},{13,5},{2,10},{6,14},... | collective-permute-start | bytes 405512 | tf_op jit(solution)/shard_map/ppermute | solution.py:263
  6.1 11.4 %collective-permute-start = (bf16[66,8,128]{2,1,0:T(8,128)(2,1)S(1)}, bf16[66,8,128]{2,1,0:T(8,128)(2,1)S(1)}, u32[]{:S(2)}, u32[]{:S(2)}) collective-permute-start(bf16[66,8,128]{2,1,0:T(8,128)(2,1)S(1)} %shard_map.64.refs_0_), channel_id=1, source_target_pairs={{0,4},{4,0},{8,12},{12,8},{1,5},{5,1},{9,13},{13,9},{2,6},{6,2},{1... | collective-permute-start | bytes 405512 | tf_op jit(solution)/shard_map/ppermute | solution.py:263
  27.2 6.5 %collective-permute-start.5 = (bf16[64,1024]{1,0:T(8,128)(2,1)S(1)}, bf16[64,1024]{1,0:T(8,128)(2,1)S(1)}, u32[]{:S(2)}, u32[]{:S(2)}) collective-permute-start(bf16[64,1024]{1,0:T(8,128)(2,1)S(1)} %get-tuple-element.22), channel_id=1, source_target_pairs={{0,4},{4,0},{8,12},{12,8},{1,5},{5,1},{9,13},{13,9},{2,6},{6,2},{1... | collective-permute-start | bytes 393224 | tf_op jit(solution)/shard_map/ppermute | solution.py:263
  27.3 12.5 %collective-permute-start.3 = (bf16[64,1024]{1,0:T(8,128)(2,1)S(1)}, bf16[64,1024]{1,0:T(8,128)(2,1)S(1)}, u32[]{:S(2)}, u32[]{:S(2)}) collective-permute-start(bf16[64,1024]{1,0:T(8,128)(2,1)S(1)} %get-tuple-element.20), channel_id=1, source_target_pairs={{0,8},{4,12},{8,0},{12,4},{1,9},{5,13},{9,1},{13,5},{2,10},{6,14},... | collective-permute-start | bytes 393224 | tf_op jit(solution)/shard_map/ppermute | solution.py:263
  30.3 9.5 %collective-permute-start.4 = (bf16[64,1024]{1,0:T(8,128)(2,1)S(1)}, bf16[64,1024]{1,0:T(8,128)(2,1)S(1)}, u32[]{:S(2)}, u32[]{:S(2)}) collective-permute-start(bf16[64,1024]{1,0:T(8,128)(2,1)S(1)} %get-tuple-element.21), channel_id=1, source_target_pairs={{0,12},{4,8},{8,4},{12,0},{1,13},{5,9},{9,5},{13,1},{2,14},{6,10},... | collective-permute-start | bytes 393224 | tf_op jit(solution)/shard_map/ppermute | solution.py:263

commit v2 on v1

--- a/solution.py
+++ b/solution.py
@@ -272,7 +272,11 @@
         got = {s: exchange(packed, pairs[s]) for s in pairs}
         gate, up, own = own_hidden(tokens, w_gate, w_up)
         parts, down, beside = far([got[2], got[3], got[1]], 2, gate, up, w_down, count, top)
-        back = [exchange(part, pairs[s]) for part, s in zip(parts, (2, 3))]
+        back = [
+            exchange(parts[1], pairs[3][1:3]),
+            exchange(parts[0], pairs[2]),
+            exchange(parts[1], pairs[3][::3]),
+        ]
         total, part = near([packed, got[1]], [own, beside], down, top)
         back.append(exchange(part, pairs[1]))
         for part in back:

time: 40.7 us -> 40.1 us (0.985)
  waiting for transfers between devices: 9.77 us -> 6.46 us
  starting transfers between devices: 10.2 us -> 12.8 us
    ppermute x6 -> x7, waiting for transfers between devices: 9.77 us -> 6.46 us  [exchange(): return lax.ppermute(array, 'expert', pairs)]
    ppermute x6 -> x7, starting transfers between devices: 10.2 us -> 12.8 us  [exchange(): return lax.ppermute(array, 'expert', pairs)]
  transfers between devices with their start and end apart: 6 -> 7, of which waited for: 3 -> 3; matrix products, arithmetic and copies ran while one was open for 0% -> 0% of each run, Pallas kernels for 23% -> 23%
where the time goes in v2:
time: 40.1 us; the launch traced here: 39.8 us
  Pallas kernels  19.8 us (49%)
  starting transfers between devices  12.8 us (32%)
  waiting for transfers between devices  6.46 us (16%)
  other arithmetic  0.75 us (2%)
    ppermute x7, starting transfers between devices, exchange(): return lax.ppermute(array, 'expert', pairs)  12.8 us
    pallas_call x1, Pallas kernels, own_hidden(): pl.pallas_call(own_kernel, out_shape=[pltpu.VMEM(w_gate.shape, w_gate.dty...  9.15 us
    pallas_call x1, Pallas kernels, far(): pl.pallas_call(functools.partial(far_kernel, blocks, sent, top), out_shap...  7.63 us
    ppermute x7, waiting for transfers between devices, exchange(): return lax.ppermute(array, 'expert', pairs)  6.46 us
    pallas_call x1, Pallas kernels, near(): pl.pallas_call(functools.partial(near_kernel, top), out_shape=[jax.ShapeD...  2.02 us
    pallas_call x1, Pallas kernels, pack(): pl.pallas_call(pack_kernel, out_shape=pltpu.VMEM((tiles.shape[0] + 2, SUB...  0.96 us
  transfers between devices with their start and end apart: 7, of which 3 were waited for; matrix products, arithmetic and copies ran while one was open for 0% of the time, Pallas kernels for 23%

profile of v2, /device:TPU:0, one launch (start us, length us, event | category | flops | bytes accessed | tf_op | source)
XLA Modules:
  0.0 39.8 jit_solution(13863896430947409001)
XLA Ops:
  0.0 1.0 %shard_map.64.refs_0_ = bf16[66,8,128]{2,1,0:T(8,128)(2,1)S(1)} custom-call(bf16[64,8,128]{2,1,0:T(8,128)(2,1)} %bitcast.7, s32[8,64]{1,0:T(8,128)} %bitcast.8, f32[8,64]{1,0:T(8,128)} %bitcast.9), custom_call_target="tpu_custom_call" | custom-call | tf_op jit(solution)/shard_map/pallas_call | solution.py:63
  1.0 5.1 %collective-permute-start.2 = (bf16[66,8,128]{2,1,0:T(8,128)(2,1)S(1)}, bf16[66,8,128]{2,1,0:T(8,128)(2,1)S(1)}, u32[]{:S(2)}, u32[]{:S(2)}) collective-permute-start(bf16[66,8,128]{2,1,0:T(8,128)(2,1)S(1)} %shard_map.64.refs_0_), channel_id=1, source_target_pairs={{0,12},{4,8},{8,4},{12,0},{1,13},{5,9},{9,5},{13,1},{2,14},{6,10},... | collective-permute-start | bytes 405512 | tf_op jit(solution)/shard_map/ppermute | solution.py:263
  6.1 0.0 collective-permute-start.1
  6.1 0.6 %collective-permute-start = (bf16[66,8,128]{2,1,0:T(8,128)(2,1)S(1)}, bf16[66,8,128]{2,1,0:T(8,128)(2,1)S(1)}, u32[]{:S(2)}, u32[]{:S(2)}) collective-permute-start(bf16[66,8,128]{2,1,0:T(8,128)(2,1)S(1)} %shard_map.64.refs_0_), channel_id=1, source_target_pairs={{0,4},{4,0},{8,12},{12,8},{1,5},{5,1},{9,13},{13,9},{2,6},{6,2},{1... | collective-permute-start | bytes 405512 | tf_op jit(solution)/shard_map/ppermute | solution.py:263
  6.8 9.2 %shard_map.65 = (bf16[8,1024,768]{2,1,0:T(8,128)(2,1)S(1)}, bf16[8,1024,768]{2,1,0:T(8,128)(2,1)S(1)}, bf16[8,64,768]{2,1,0:T(8,128)(2,1)S(1)}) custom-call(bf16[64,1024]{1,0:T(8,128)(2,1)} %token_hbm.1, bf16[8,1024,768]{2,1,0:T(8,128)(2,1)} %gate_hbm.1, bf16[8,1024,768]{2,1,0:T(8,128)(2,1)} %up_hbm.1), custom_call_target="tpu_custom_call" | custom-call | flops 1610612736 | bytes 25165824 | tf_op jit(solution)/shard_map/pallas_call | solution.py:105
  15.9 0.0 collective-permute-done.2.refs_1_
  15.9 1.6 %collective-permute-done.1.refs_0_ = bf16[66,8,128]{2,1,0:T(8,128)(2,1)S(1)} collective-permute-done((bf16[66,8,128]{2,1,0:T(8,128)(2,1)S(1)}, bf16[66,8,128]{2,1,0:T(8,128)(2,1)S(1)}, u32[]{:S(2)}, u32[]{:S(2)}) %collective-permute-start.1) | collective-permute-done | bytes 135200 | tf_op jit(solution)/shard_map/ppermute | solution.py:263
  17.5 0.0 collective-permute-done.refs_2_.refs_1_
  17.5 7.6 %shard_map.66 = (bf16[64,1024]{1,0:T(8,128)(2,1)S(1)}, bf16[64,1024]{1,0:T(8,128)(2,1)S(1)}, bf16[8,768,1024]{2,1,0:T(8,128)(2,1)S(1)}, bf16[8,64,768]{2,1,0:T(8,128)(2,1)S(1)}) custom-call(bf16[66,8,128]{2,1,0:T(8,128)(2,1)S(1)} %collective-permute-done.1.refs_0_, bf16[66,8,128]{2,1,0:T(8,128)(2,1)S(1)} %collective-permute-done.2.refs_1_, ...), custom_call_target="tpu_custom_call" | custom-call | flops 7247757312 | bytes 12582912 | tf_op jit(solution)/shard_map/pallas_call | solution.py:202
  25.2 2.0 %shard_map.67 = (f32[64,1024]{1,0:T(8,128)S(1)}, bf16[64,1024]{1,0:T(8,128)(2,1)S(1)}) custom-call(bf16[66,8,128]{2,1,0:T(8,128)(2,1)S(1)} %shard_map.64.refs_0_, bf16[66,8,128]{2,1,0:T(8,128)(2,1)S(1)} %collective-permute-done.refs_2_.refs_1_, bf16[8,64,768]{2,1,0:T(8,128)(2,1)S(1)} %get-tuple-element.14.refs_2_, ...), custom_call_target="tpu_custom_call" | custom-call | flops 1610612736 | bytes 12582912 | tf_op jit(solution)/shard_map/pallas_call | solution.py:242
  27.2 0.1 collective-permute-start.6
  27.3 3.1 %collective-permute-start.4 = (bf16[64,1024]{1,0:T(8,128)(2,1)S(1)}, bf16[64,1024]{1,0:T(8,128)(2,1)S(1)}, u32[]{:S(2)}, u32[]{:S(2)}) collective-permute-start(bf16[64,1024]{1,0:T(8,128)(2,1)S(1)} %get-tuple-element.21), channel_id=1, source_target_pairs={{0,8},{4,12},{8,0},{12,4},{1,9},{5,13},{9,1},{13,5},{2,10},{6,14},... | collective-permute-start | bytes 393224 | tf_op jit(solution)/shard_map/ppermute | solution.py:263
  30.3 3.2 %collective-permute-start.5 = (bf16[64,1024]{1,0:T(8,128)(2,1)S(1)}, bf16[64,1024]{1,0:T(8,128)(2,1)S(1)}, u32[]{:S(2)}, u32[]{:S(2)}) collective-permute-start(bf16[64,1024]{1,0:T(8,128)(2,1)S(1)} %get-tuple-element.20), channel_id=1, source_target_pairs={{0,12},{12,0},{1,13},{13,1},{2,14},{14,2},{3,15},{15,3},{16,28},{2... | collective-permute-start | bytes 393224 | tf_op jit(solution)/shard_map/ppermute | solution.py:263
  33.6 0.7 %collective-permute-start.3 = (bf16[64,1024]{1,0:T(8,128)(2,1)S(1)}, bf16[64,1024]{1,0:T(8,128)(2,1)S(1)}, u32[]{:S(2)}, u32[]{:S(2)}) collective-permute-start(bf16[64,1024]{1,0:T(8,128)(2,1)S(1)} %get-tuple-element.20), channel_id=1, source_target_pairs={{4,8},{8,4},{5,9},{9,5},{6,10},{10,6},{7,11},{11,7},{20,24},{24,20... | collective-permute-start | bytes 393224 | tf_op jit(solution)/shard_map/ppermute | solution.py:263
  34.2 0.0 collective-permute-done.6
  34.3 3.4 %collective-permute-done.4 = bf16[64,1024]{1,0:T(8,128)(2,1)S(1)} collective-permute-done((bf16[64,1024]{1,0:T(8,128)(2,1)S(1)}, bf16[64,1024]{1,0:T(8,128)(2,1)S(1)}, u32[]{:S(2)}, u32[]{:S(2)}) %collective-permute-start.4) | collective-permute-done | bytes 131104 | tf_op jit(solution)/shard_map/ppermute | solution.py:263
  37.7 1.4 %collective-permute-done.5 = bf16[64,1024]{1,0:T(8,128)(2,1)S(1)} collective-permute-done((bf16[64,1024]{1,0:T(8,128)(2,1)S(1)}, bf16[64,1024]{1,0:T(8,128)(2,1)S(1)}, u32[]{:S(2)}, u32[]{:S(2)}) %collective-permute-start.5) | collective-permute-done | bytes 131104 | tf_op jit(solution)/shard_map/ppermute | solution.py:263
  39.1 0.0 collective-permute-done.3
  39.1 0.7 %add_convert_fusion = bf16[64,1024]{1,0:T(8,128)(2,1)} fusion(bf16[64,1024]{1,0:T(8,128)(2,1)S(1)} %collective-permute-done.6, bf16[64,1024]{1,0:T(8,128)(2,1)S(1)} %collective-permute-done.5, bf16[64,1024]{1,0:T(8,128)(2,1)S(1)} %collective-permute-done.4, f32[64,1024]{1,0:T(8,128)S(1)} %get-tuple-element.19, bf16[64,1024]{1,0:T(8,128)(2,1)S(1)} %collective-permute-done.3), kind=kLoop, calls=%fused_computation | loop fusion | flops 589824 | bytes 917504 | tf_op jit(solution)/shard_map/convert_element_type | solution.py:284
Async XLA Ops:
  1.0 15.0 %collective-permute-start.2 = (bf16[66,8,128]{2,1,0:T(8,128)(2,1)S(1)}, bf16[66,8,128]{2,1,0:T(8,128)(2,1)S(1)}, u32[]{:S(2)}, u32[]{:S(2)}) collective-permute-start(bf16[66,8,128]{2,1,0:T(8,128)(2,1)S(1)} %shard_map.64.refs_0_), channel_id=1, source_target_pairs={{0,12},{4,8},{8,4},{12,0},{1,13},{5,9},{9,5},{13,1},{2,14},{6,10},... | collective-permute-start | bytes 405512 | tf_op jit(solution)/shard_map/ppermute | solution.py:263
  6.1 11.4 %collective-permute-start.1 = (bf16[66,8,128]{2,1,0:T(8,128)(2,1)S(1)}, bf16[66,8,128]{2,1,0:T(8,128)(2,1)S(1)}, u32[]{:S(2)}, u32[]{:S(2)}) collective-permute-start(bf16[66,8,128]{2,1,0:T(8,128)(2,1)S(1)} %shard_map.64.refs_0_), channel_id=1, source_target_pairs={{0,8},{4,12},{8,0},{12,4},{1,9},{5,13},{9,1},{13,5},{2,10},{6,14},... | collective-permute-start | bytes 405512 | tf_op jit(solution)/shard_map/ppermute | solution.py:263
  6.1 11.4 %collective-permute-start = (bf16[66,8,128]{2,1,0:T(8,128)(2,1)S(1)}, bf16[66,8,128]{2,1,0:T(8,128)(2,1)S(1)}, u32[]{:S(2)}, u32[]{:S(2)}) collective-permute-start(bf16[66,8,128]{2,1,0:T(8,128)(2,1)S(1)} %shard_map.64.refs_0_), channel_id=1, source_target_pairs={{0,4},{4,0},{8,12},{12,8},{1,5},{5,1},{9,13},{13,9},{2,6},{6,2},{1... | collective-permute-start | bytes 405512 | tf_op jit(solution)/shard_map/ppermute | solution.py:263
  27.2 7.0 %collective-permute-start.6 = (bf16[64,1024]{1,0:T(8,128)(2,1)S(1)}, bf16[64,1024]{1,0:T(8,128)(2,1)S(1)}, u32[]{:S(2)}, u32[]{:S(2)}) collective-permute-start(bf16[64,1024]{1,0:T(8,128)(2,1)S(1)} %get-tuple-element.22), channel_id=1, source_target_pairs={{0,4},{4,0},{8,12},{12,8},{1,5},{5,1},{9,13},{13,9},{2,6},{6,2},{1... | collective-permute-start | bytes 393224 | tf_op jit(solution)/shard_map/ppermute | solution.py:263
  27.3 10.4 %collective-permute-start.4 = (bf16[64,1024]{1,0:T(8,128)(2,1)S(1)}, bf16[64,1024]{1,0:T(8,128)(2,1)S(1)}, u32[]{:S(2)}, u32[]{:S(2)}) collective-permute-start(bf16[64,1024]{1,0:T(8,128)(2,1)S(1)} %get-tuple-element.21), channel_id=1, source_target_pairs={{0,8},{4,12},{8,0},{12,4},{1,9},{5,13},{9,1},{13,5},{2,10},{6,14},... | collective-permute-start | bytes 393224 | tf_op jit(solution)/shard_map/ppermute | solution.py:263
  30.3 8.8 %collective-permute-start.5 = (bf16[64,1024]{1,0:T(8,128)(2,1)S(1)}, bf16[64,1024]{1,0:T(8,128)(2,1)S(1)}, u32[]{:S(2)}, u32[]{:S(2)}) collective-permute-start(bf16[64,1024]{1,0:T(8,128)(2,1)S(1)} %get-tuple-element.20), channel_id=1, source_target_pairs={{0,12},{12,0},{1,13},{13,1},{2,14},{14,2},{3,15},{15,3},{16,28},{2... | collective-permute-start | bytes 393224 | tf_op jit(solution)/shard_map/ppermute | solution.py:263
  33.6 5.5 %collective-permute-start.3 = (bf16[64,1024]{1,0:T(8,128)(2,1)S(1)}, bf16[64,1024]{1,0:T(8,128)(2,1)S(1)}, u32[]{:S(2)}, u32[]{:S(2)}) collective-permute-start(bf16[64,1024]{1,0:T(8,128)(2,1)S(1)} %get-tuple-element.20), channel_id=1, source_target_pairs={{4,8},{8,4},{5,9},{9,5},{6,10},{10,6},{7,11},{11,7},{20,24},{24,20... | collective-permute-start | bytes 393224 | tf_op jit(solution)/shard_map/ppermute | solution.py:263

commit v3 on v1

--- a/solution.py
+++ b/solution.py
@@ -223,10 +223,11 @@
     return parts, down, near_hidden
 
 
-def near_kernel(top, *refs):
-    packed_refs, hidden_refs, down_ref = refs[:2], refs[2:4], refs[4]
-    out_refs = refs[5:7]
-    spread_ref, hidden_ref, total_ref = refs[7:]
+def near_kernel(blocks, top, *refs):
+    packed_refs, hidden_refs = refs[:blocks], refs[blocks : blocks + 2]
+    down_ref = refs[blocks + 2]
+    out_refs = refs[blocks + 3 : 2 * blocks + 3]
+    spread_ref, hidden_ref, total_ref = refs[2 * blocks + 3 :]
     count = hidden_refs[0].shape[1]
     spread_shares(packed_refs, spread_ref, count, top, down_ref.shape[0])
     hidden_ref[:, :count, :] = hidden_refs[0][...]
@@ -236,25 +237,24 @@
     )
 
 
-def near(packed, hiddens, down, top):
+def near(packed, hiddens, down, kinds, top):
+    blocks = len(packed)
     local_experts, count, units = hiddens[0].shape
     width = down.shape[2]
+    rows = blocks * count
     return pl.pallas_call(
-        functools.partial(near_kernel, top),
-        out_shape=[
-            jax.ShapeDtypeStruct((count, width), jnp.float32),
-            jax.ShapeDtypeStruct((count, width), jnp.bfloat16),
-        ],
-        in_specs=[VMEM] * 5,
-        out_specs=[VMEM] * 2,
+        functools.partial(near_kernel, blocks, top),
+        out_shape=[jax.ShapeDtypeStruct((count, width), kind) for kind in kinds],
+        in_specs=[VMEM] * (blocks + 3),
+        out_specs=[VMEM] * blocks,
         scratch_shapes=[
-            pltpu.VMEM((2 * count, slots_of(local_experts)), jnp.float32),
-            pltpu.VMEM((local_experts, 2 * count, units), jnp.bfloat16),
-            pltpu.VMEM((2 * count, width), jnp.float32),
-        ],
-        compiler_params=pltpu.CompilerParams(vmem_limit_bytes=8 * MIB),
+            pltpu.VMEM((rows, slots_of(local_experts)), jnp.float32),
+            pltpu.VMEM((local_experts, rows, units), jnp.bfloat16),
+            pltpu.VMEM((rows, width), jnp.float32),
+        ],
+        compiler_params=pltpu.CompilerParams(vmem_limit_bytes=10 * MIB),
         cost_estimate=pl.CostEstimate(
-            flops=4 * count * down.size, bytes_accessed=2 * down.size, transcendentals=0
+            flops=2 * rows * down.size, bytes_accessed=2 * down.size, transcendentals=0
         ),
     )(*packed, *hiddens, down)
 
@@ -271,10 +271,13 @@
         pairs = {shift: [(i, i ^ shift) for i in range(peers)] for shift in (2, 3, 1)}
         got = {s: exchange(packed, pairs[s]) for s in pairs}
         gate, up, own = own_hidden(tokens, w_gate, w_up)
-        parts, down, beside = far([got[2], got[3], got[1]], 2, gate, up, w_down, count, top)
-        back = [exchange(part, pairs[s]) for part, s in zip(parts, (2, 3))]
-        total, part = near([packed, got[1]], [own, beside], down, top)
-        back.append(exchange(part, pairs[1]))
+        order = [got[3], got[2], got[1]]
+        parts, down, beside = far(order, 1, gate, up, w_down, count, top)
+        hop = exchange(parts[0], pairs[1])
+        kinds = (jnp.float32, jnp.float32, jnp.bfloat16)
+        total, part, beside_part = near([packed, got[2], got[1]], [own, beside], down, kinds, top)
+        both = (part + hop.astype(jnp.float32)).astype(jnp.bfloat16)
+        back = [exchange(both, pairs[2]), exchange(beside_part, pairs[1])]
         for part in back:
             total = total + part.astype(jnp.float32)
         return total.astype(jnp.bfloat16)

time: 40.7 us -> 39.1 us (0.961)
  waiting for transfers between devices: 9.77 us -> 8.31 us
  starting transfers between devices: 10.2 us -> 9 us
  Pallas kernels: 19.8 us -> 20.8 us
    ppermute x6, waiting for transfers between devices: 9.77 us -> 8.31 us  [exchange(): return lax.ppermute(array, 'expert', pairs)]
    ppermute x6, starting transfers between devices: 10.2 us -> 9 us  [exchange(): return lax.ppermute(array, 'expert', pairs)]
    pallas_call x1, Pallas kernels: 2.02 us -> 2.8 us  [near(): pl.pallas_call(functools.partial(near_kernel, blocks, top), out_shape=[ja...]
  transfers between devices with their start and end apart: 6 -> 6, of which waited for: 3 -> 4; matrix products, arithmetic and copies ran while one was open for 0% -> 0% of each run, Pallas kernels for 23% -> 31%
where the time goes in v3:
time: 39.1 us; the launch traced here: 38.9 us
  Pallas kernels  20.8 us (53%)
  starting transfers between devices  9 us (23%)
  waiting for transfers between devices  8.31 us (21%)
  other arithmetic  0.73 us (2%)
    pallas_call x1, Pallas kernels, own_hidden(): pl.pallas_call(own_kernel, out_shape=[pltpu.VMEM(w_gate.shape, w_gate.dty...  9.15 us
    ppermute x6, starting transfers between devices, exchange(): return lax.ppermute(array, 'expert', pairs)  9 us
    ppermute x6, waiting for transfers between devices, exchange(): return lax.ppermute(array, 'expert', pairs)  8.31 us
    pallas_call x1, Pallas kernels, far(): pl.pallas_call(functools.partial(far_kernel, blocks, sent, top), out_shap...  7.85 us
    pallas_call x1, Pallas kernels, near(): pl.pallas_call(functools.partial(near_kernel, blocks, top), out_shape=[ja...  2.8 us
    pallas_call x1, Pallas kernels, pack(): pl.pallas_call(pack_kernel, out_shape=pltpu.VMEM((tiles.shape[0] + 2, SUB...  0.96 us
  transfers between devices with their start and end apart: 6, of which 4 were waited for; matrix products, arithmetic and copies ran while one was open for 0% of the time, Pallas kernels for 31%

profile of v3, /device:TPU:0, one launch (start us, length us, event | category | flops | bytes accessed | tf_op | source)
XLA Modules:
  0.0 38.9 jit_solution(16846367996498664283)
XLA Ops:
  0.0 1.0 %shard_map.64.refs_0_ = bf16[66,8,128]{2,1,0:T(8,128)(2,1)S(1)} custom-call(bf16[64,8,128]{2,1,0:T(8,128)(2,1)} %bitcast.7, s32[8,64]{1,0:T(8,128)} %bitcast.8, f32[8,64]{1,0:T(8,128)} %bitcast.9), custom_call_target="tpu_custom_call" | custom-call | tf_op jit(solution)/shard_map/pallas_call | solution.py:63
  1.0 5.1 %collective-permute-start.2 = (bf16[66,8,128]{2,1,0:T(8,128)(2,1)S(1)}, bf16[66,8,128]{2,1,0:T(8,128)(2,1)S(1)}, u32[]{:S(2)}, u32[]{:S(2)}) collective-permute-start(bf16[66,8,128]{2,1,0:T(8,128)(2,1)S(1)} %shard_map.64.refs_0_), channel_id=1, source_target_pairs={{0,12},{4,8},{8,4},{12,0},{1,13},{5,9},{9,5},{13,1},{2,14},{6,10},... | collective-permute-start | bytes 405512 | tf_op jit(solution)/shard_map/ppermute | solution.py:263
  6.1 0.0 collective-permute-start.1
  6.1 0.6 %collective-permute-start = (bf16[66,8,128]{2,1,0:T(8,128)(2,1)S(1)}, bf16[66,8,128]{2,1,0:T(8,128)(2,1)S(1)}, u32[]{:S(2)}, u32[]{:S(2)}) collective-permute-start(bf16[66,8,128]{2,1,0:T(8,128)(2,1)S(1)} %shard_map.64.refs_0_), channel_id=1, source_target_pairs={{0,8},{4,12},{8,0},{12,4},{1,9},{5,13},{9,1},{13,5},{2,10},{6,14},... | collective-permute-start | bytes 405512 | tf_op jit(solution)/shard_map/ppermute | solution.py:263
  6.8 9.2 %shard_map.65 = (bf16[8,1024,768]{2,1,0:T(8,128)(2,1)S(1)}, bf16[8,1024,768]{2,1,0:T(8,128)(2,1)S(1)}, bf16[8,64,768]{2,1,0:T(8,128)(2,1)S(1)}) custom-call(bf16[64,1024]{1,0:T(8,128)(2,1)} %token_hbm.1, bf16[8,1024,768]{2,1,0:T(8,128)(2,1)} %gate_hbm.1, bf16[8,1024,768]{2,1,0:T(8,128)(2,1)} %up_hbm.1), custom_call_target="tpu_custom_call" | custom-call | flops 1610612736 | bytes 25165824 | tf_op jit(solution)/shard_map/pallas_call | solution.py:105
  15.9 0.0 collective-permute-done.2.refs_0_
  15.9 0.0 collective-permute-done.1.refs_2_
  15.9 1.6 %collective-permute-done.refs_1_ = bf16[66,8,128]{2,1,0:T(8,128)(2,1)S(1)} collective-permute-done((bf16[66,8,128]{2,1,0:T(8,128)(2,1)S(1)}, bf16[66,8,128]{2,1,0:T(8,128)(2,1)S(1)}, u32[]{:S(2)}, u32[]{:S(2)}) %collective-permute-start) | collective-permute-done | bytes 135200 | tf_op jit(solution)/shard_map/ppermute | solution.py:263
  17.5 7.8 %shard_map.66 = (bf16[64,1024]{1,0:T(8,128)(2,1)S(1)}, bf16[8,768,1024]{2,1,0:T(8,128)(2,1)S(1)}, bf16[8,128,768]{2,1,0:T(8,128)(2,1)S(1)}) custom-call(bf16[66,8,128]{2,1,0:T(8,128)(2,1)S(1)} %collective-permute-done.2.refs_0_, bf16[66,8,128]{2,1,0:T(8,128)(2,1)S(1)} %collective-permute-done.refs_1_, ...), custom_call_target="tpu_custom_call" | custom-call | flops 7247757312 | bytes 12582912 | tf_op jit(solution)/shard_map/pallas_call | solution.py:202
  25.4 0.1 collective-permute-start.3
  25.5 2.8 %shard_map.67 = (f32[64,1024]{1,0:T(8,128)S(1)}, f32[64,1024]{1,0:T(8,128)S(1)}, bf16[64,1024]{1,0:T(8,128)(2,1)S(1)}) custom-call(bf16[66,8,128]{2,1,0:T(8,128)(2,1)S(1)} %shard_map.64.refs_0_, bf16[66,8,128]{2,1,0:T(8,128)(2,1)S(1)} %collective-permute-done.refs_1_, bf16[66,8,128]{2,1,0:T(8,128)(2,1)S(1)} %collective-permute-done.1.refs_2_, ...), custom_call_target="tpu_custom_call" | custom-call | flops 2415919104 | bytes 12582912 | tf_op jit(solution)/shard_map/pallas_call | solution.py:245
  28.3 2.1 %collective-permute-start.5 = (bf16[64,1024]{1,0:T(8,128)(2,1)S(1)}, bf16[64,1024]{1,0:T(8,128)(2,1)S(1)}, u32[]{:S(2)}, u32[]{:S(2)}) collective-permute-start(bf16[64,1024]{1,0:T(8,128)(2,1)S(1)} %get-tuple-element.22), channel_id=1, source_target_pairs={{0,4},{4,0},{8,12},{12,8},{1,5},{5,1},{9,13},{13,9},{2,6},{6,2},{1... | collective-permute-start | bytes 393224 | tf_op jit(solution)/shard_map/ppermute | solution.py:263
  30.4 0.4 collective-permute-done.3
  30.8 1.1 %collective-permute-start.4 = (bf16[64,1024]{1,0:T(8,128)(2,1)S(1)}, bf16[64,1024]{1,0:T(8,128)(2,1)S(1)}, u32[]{:S(2)}, u32[]{:S(2)}) collective-permute-start(bf16[64,1024]{1,0:T(8,128)(2,1)S(1)} %add_convert_fusion.1), channel_id=1, source_target_pairs={{0,8},{4,12},{8,0},{12,4},{1,9},{5,13},{9,1},{13,5},{2,10},{6,14},... | collective-permute-start | bytes 393224 | tf_op jit(solution)/shard_map/ppermute | solution.py:263
  31.8 2.3 %collective-permute-done.5 = bf16[64,1024]{1,0:T(8,128)(2,1)S(1)} collective-permute-done((bf16[64,1024]{1,0:T(8,128)(2,1)S(1)}, bf16[64,1024]{1,0:T(8,128)(2,1)S(1)}, u32[]{:S(2)}, u32[]{:S(2)}) %collective-permute-start.5) | collective-permute-done | bytes 131104 | tf_op jit(solution)/shard_map/ppermute | solution.py:263
  34.1 4.1 %collective-permute-done.4 = bf16[64,1024]{1,0:T(8,128)(2,1)S(1)} collective-permute-done((bf16[64,1024]{1,0:T(8,128)(2,1)S(1)}, bf16[64,1024]{1,0:T(8,128)(2,1)S(1)}, u32[]{:S(2)}, u32[]{:S(2)}) %collective-permute-start.4) | collective-permute-done | bytes 131104 | tf_op jit(solution)/shard_map/ppermute | solution.py:263
  38.2 0.7 %add_convert_fusion = bf16[64,1024]{1,0:T(8,128)(2,1)} fusion(bf16[64,1024]{1,0:T(8,128)(2,1)S(1)} %collective-permute-done.5, f32[64,1024]{1,0:T(8,128)S(1)} %get-tuple-element.19, bf16[64,1024]{1,0:T(8,128)(2,1)S(1)} %collective-permute-done.4), kind=kLoop, calls=%fused_computation | loop fusion | flops 327680 | bytes 655360 | tf_op jit(solution)/shard_map/convert_element_type | solution.py:283
  (1 shorter events, 0.0 us)
Async XLA Ops:
  1.0 15.0 %collective-permute-start.2 = (bf16[66,8,128]{2,1,0:T(8,128)(2,1)S(1)}, bf16[66,8,128]{2,1,0:T(8,128)(2,1)S(1)}, u32[]{:S(2)}, u32[]{:S(2)}) collective-permute-start(bf16[66,8,128]{2,1,0:T(8,128)(2,1)S(1)} %shard_map.64.refs_0_), channel_id=1, source_target_pairs={{0,12},{4,8},{8,4},{12,0},{1,13},{5,9},{9,5},{13,1},{2,14},{6,10},... | collective-permute-start | bytes 405512 | tf_op jit(solution)/shard_map/ppermute | solution.py:263
  6.1 9.8 %collective-permute-start.1 = (bf16[66,8,128]{2,1,0:T(8,128)(2,1)S(1)}, bf16[66,8,128]{2,1,0:T(8,128)(2,1)S(1)}, u32[]{:S(2)}, u32[]{:S(2)}) collective-permute-start(bf16[66,8,128]{2,1,0:T(8,128)(2,1)S(1)} %shard_map.64.refs_0_), channel_id=1, source_target_pairs={{0,4},{4,0},{8,12},{12,8},{1,5},{5,1},{9,13},{13,9},{2,6},{6,2},{1... | collective-permute-start | bytes 405512 | tf_op jit(solution)/shard_map/ppermute | solution.py:263
  6.1 11.4 %collective-permute-start = (bf16[66,8,128]{2,1,0:T(8,128)(2,1)S(1)}, bf16[66,8,128]{2,1,0:T(8,128)(2,1)S(1)}, u32[]{:S(2)}, u32[]{:S(2)}) collective-permute-start(bf16[66,8,128]{2,1,0:T(8,128)(2,1)S(1)} %shard_map.64.refs_0_), channel_id=1, source_target_pairs={{0,8},{4,12},{8,0},{12,4},{1,9},{5,13},{9,1},{13,5},{2,10},{6,14},... | collective-permute-start | bytes 405512 | tf_op jit(solution)/shard_map/ppermute | solution.py:263
  25.4 5.4 %collective-permute-start.3 = (bf16[64,1024]{1,0:T(8,128)(2,1)S(1)}, bf16[64,1024]{1,0:T(8,128)(2,1)S(1)}, u32[]{:S(2)}, u32[]{:S(2)}) collective-permute-start(bf16[64,1024]{1,0:T(8,128)(2,1)S(1)} %get-tuple-element.21), channel_id=1, source_target_pairs={{0,4},{4,0},{8,12},{12,8},{1,5},{5,1},{9,13},{13,9},{2,6},{6,2},{1... | collective-permute-start | bytes 393224 | tf_op jit(solution)/shard_map/ppermute | solution.py:263
  28.3 5.8 %collective-permute-start.5 = (bf16[64,1024]{1,0:T(8,128)(2,1)S(1)}, bf16[64,1024]{1,0:T(8,128)(2,1)S(1)}, u32[]{:S(2)}, u32[]{:S(2)}) collective-permute-start(bf16[64,1024]{1,0:T(8,128)(2,1)S(1)} %get-tuple-element.22), channel_id=1, source_target_pairs={{0,4},{4,0},{8,12},{12,8},{1,5},{5,1},{9,13},{13,9},{2,6},{6,2},{1... | collective-permute-start | bytes 393224 | tf_op jit(solution)/shard_map/ppermute | solution.py:263
  30.8 7.4 %collective-permute-start.4 = (bf16[64,1024]{1,0:T(8,128)(2,1)S(1)}, bf16[64,1024]{1,0:T(8,128)(2,1)S(1)}, u32[]{:S(2)}, u32[]{:S(2)}) collective-permute-start(bf16[64,1024]{1,0:T(8,128)(2,1)S(1)} %add_convert_fusion.1), channel_id=1, source_target_pairs={{0,8},{4,12},{8,0},{12,4},{1,9},{5,13},{9,1},{13,5},{2,10},{6,14},... | collective-permute-start | bytes 393224 | tf_op jit(solution)/shard_map/ppermute | solution.py:263

commit v4 on v3

--- a/solution.py
+++ b/solution.py
@@ -74,7 +74,7 @@
     )(in_hbm(tiles), in_hbm(expert_ids.T), in_hbm(route_scores.T))
 
 
-def own_kernel(token_hbm, gate_hbm, up_hbm, gate_ref, up_ref, hidden_ref, rows_ref, sems):
+def own_kernel(begin, token_hbm, gate_hbm, up_hbm, gate_ref, up_ref, hidden_ref, rows_ref, sems):
     local_experts = gate_ref.shape[0]
     tokens = pltpu.make_async_copy(token_hbm, rows_ref, sems.at[2, 0])
     tokens.start()
@@ -82,7 +82,7 @@
     def load(member, which):
         source, target = ((gate_hbm, gate_ref), (up_hbm, up_ref))[which]
         return pltpu.make_async_copy(
-            source.at[member], target.at[member], sems.at[which, member]
+            source.at[begin + member], target.at[member], sems.at[which, member]
         )
 
     for member in range(local_experts):
@@ -99,25 +99,28 @@
     lax.fori_loop(0, local_experts, one_expert, 0)
 
 
-def own_hidden(tokens, w_gate, w_up):
-    local_experts, _, units = w_gate.shape
+def own_hidden(tokens, w_gate, w_up, begin, end):
+    _, width, units = w_gate.shape
+    held = end - begin
     count = tokens.shape[0]
     return pl.pallas_call(
-        own_kernel,
+        functools.partial(own_kernel, begin),
         out_shape=[
-            pltpu.VMEM(w_gate.shape, w_gate.dtype),
-            pltpu.VMEM(w_up.shape, w_up.dtype),
-            pltpu.VMEM((local_experts, count, units), jnp.bfloat16),
+            pltpu.VMEM((held, width, units), w_gate.dtype),
+            pltpu.VMEM((held, width, units), w_up.dtype),
+            pltpu.VMEM((held, count, units), jnp.bfloat16),
         ],
         in_specs=[ANY] * 3,
         out_specs=[VMEM] * 3,
         scratch_shapes=[
             pltpu.VMEM(tokens.shape, tokens.dtype),
-            pltpu.SemaphoreType.DMA((3, local_experts)),
+            pltpu.SemaphoreType.DMA((3, held)),
         ],
         compiler_params=pltpu.CompilerParams(vmem_limit_bytes=8 * MIB),
         cost_estimate=pl.CostEstimate(
-            flops=4 * count * w_gate.size, bytes_accessed=4 * w_gate.size, transcendentals=0
+            flops=4 * count * held * width * units,
+            bytes_accessed=4 * held * width * units,
+            transcendentals=0,
         ),
     )(in_hbm(tokens), in_hbm(w_gate), in_hbm(w_up))
 
@@ -137,9 +140,11 @@
         spread_ref[index * count : (index + 1) * count, :] = spread.T
 
 
-def project_into(out_refs, total_ref, spread_ref, down_ref, hidden_at, count):
+def project_into(out_refs, total_ref, spread_ref, down_ref, hidden_at, count, before=None):
     local_experts, _, width = down_ref.shape
     for member in range(local_experts):
+        if before is not None:
+            before(member)
         weight = spread_ref[:, member : member + 1]
         for start in range(0, width, CHUNK):
             span = slice(start, min(start + CHUNK, width))
@@ -156,19 +161,33 @@
                 out_ref[:, span] = part.astype(out_ref.dtype)
 
 
-def far_kernel(blocks, sent, top, *refs):
-    packed_refs = refs[:blocks]
-    gate_ref, up_ref, down_hbm = refs[blocks : blocks + 3]
-    outs = refs[blocks + 3 :]
-    out_refs, down_ref, near_ref = outs[:sent], outs[sent], outs[sent + 1]
-    rows_ref, spread_ref, hidden_ref, total_ref, sems = outs[sent + 2 :]
-    local_experts, width, units = gate_ref.shape
-    count = rows_ref.shape[0] // blocks
+def far_kernel(blocks, sent, pieces, late, top, *refs):
+    packed_refs, refs = refs[:blocks], refs[blocks:]
+    gate_refs, up_refs, refs = refs[:pieces], refs[pieces : 2 * pieces], refs[2 * pieces :]
+    gate_hbm, up_hbm, down_hbm, *refs = refs
+    out_refs, refs = refs[:sent], refs[sent:]
+    down_ref, near_ref, own_ref, *refs = refs
+    rows_ref, spread_ref, hidden_ref, total_ref, late_ref, sems, late_sems = refs
+    local_experts, _, width = down_ref.shape
+    units = down_ref.shape[1]
+    count = own_ref.shape[1]
+    received = blocks - 1 if late else blocks
     across = width // LANES
     tiles = packed_refs[0].shape[0] - 2
+    early = local_experts - late
 
     def load(member):
         return pltpu.make_async_copy(down_hbm.at[member], down_ref.at[member], sems.at[member])
+
+    def load_late(index, which):
+        source = (gate_hbm, up_hbm)[which].at[early + index]
+        return pltpu.make_async_copy(
+            source, late_ref.at[which, index], late_sems.at[which, index]
+        )
+
+    for index in range(late):
+        load_late(index, 0).start()
+        load_late(index, 1).start()
 
     @pl.loop(0, local_experts)
     def _(member):
@@ -180,72 +199,105 @@
             column = tile % across * LANES
             rows_ref[row : row + SUBLANES, column : column + LANES] = packed_refs[index][tile]
     spread_shares(packed_refs[:sent], spread_ref, count, top, local_experts)
+    gates = [ref.at[index] for ref in gate_refs for index in range(ref.shape[0])]
+    ups = [ref.at[index] for ref in up_refs for index in range(ref.shape[0])]
+    gates += [late_ref.at[0, index] for index in range(late)]
+    ups += [late_ref.at[1, index] for index in range(late)]
     for member in range(local_experts):
+        rows = received * count
+        if member >= early:
+            load_late(member - early, 0).wait()
+            load_late(member - early, 1).wait()
+            rows = blocks * count
         for start in range(0, units, CHUNK):
             span = slice(start, min(start + CHUNK, units))
-            hidden = hidden_of(rows_ref[...], gate_ref[member, :, span], up_ref[member, :, span])
+            hidden = hidden_of(rows_ref[:rows, :], gates[member][:, span], ups[member][:, span])
             hidden_ref[member, :, span] = hidden[: sent * count]
-            if sent < blocks:
-                near_ref[member, :, span] = hidden[sent * count :]
-    for member in range(local_experts):
-        load(member).wait()
+            if sent < received:
+                near_ref[member, :, span] = hidden[sent * count : received * count]
+            if member >= early:
+                own_ref[member - early, :, span] = hidden[received * count :]
+    half = max(local_experts // 2, 1)
+
+    def arrived(member):
+        if member % half == 0:
+            for other in range(member, min(member + half, local_experts)):
+                load(other).wait()
+
     project_into(
-        out_refs, total_ref, spread_ref, down_ref, lambda member: hidden_ref[member], count
+        out_refs,
+        total_ref,
+        spread_ref,
+        down_ref,
+        lambda member: hidden_ref[member],
+        count,
+        arrived,
     )
 
 
-def far(packed, sent, gate, up, w_down, count, top):
+def far(packed, sent, gates, ups, weights, late, count, top):
+    w_gate, w_up, w_down = weights
     blocks = len(packed)
     local_experts, units, width = w_down.shape
     rows = blocks * count
-    near_rows = max(rows - sent * count, SUBLANES)
-    *parts, down, near_hidden = pl.pallas_call(
-        functools.partial(far_kernel, blocks, sent, top),
+    received = blocks - 1 if late else blocks
+    near_rows = max((received - sent) * count, SUBLANES)
+    some = max(late, 1)
+    *parts, down, near_hidden, own = pl.pallas_call(
+        functools.partial(far_kernel, blocks, sent, len(gates), late, top),
         out_shape=[jax.ShapeDtypeStruct((count, width), jnp.bfloat16)] * sent
         + [
             pltpu.VMEM(w_down.shape, w_down.dtype),
             pltpu.VMEM((local_experts, near_rows, units), jnp.bfloat16),
-        ],
-        in_specs=[VMEM] * (blocks + 2) + [ANY],
-        out_specs=[VMEM] * (sent + 2),
+            pltpu.VMEM((some, count, units), jnp.bfloat16),
+        ],
+        in_specs=[VMEM] * (blocks + 2 * len(gates)) + [ANY] * 3,
+        out_specs=[VMEM] * (sent + 3),
         scratch_shapes=[
             pltpu.VMEM((rows, width), jnp.bfloat16),
             pltpu.VMEM((sent * count, slots_of(local_experts)), jnp.float32),
             pltpu.VMEM((local_experts, sent * count, units), jnp.bfloat16),
             pltpu.VMEM((sent * count, width), jnp.float32),
+            pltpu.VMEM((2, some, width, units), jnp.bfloat16),
             pltpu.SemaphoreType.DMA((local_experts,)),
-        ],
-        compiler_params=pltpu.CompilerParams(vmem_limit_bytes=12 * MIB),
+            pltpu.SemaphoreType.DMA((2, some)),
+        ],
+        compiler_params=pltpu.CompilerParams(vmem_limit_bytes=14 * MIB),
         cost_estimate=pl.CostEstimate(
             flops=6 * rows * w_down.size, bytes_accessed=2 * w_down.size, transcendentals=0
         ),
-    )(*packed, gate, up, in_hbm(w_down))
-    return parts, down, near_hidden
-
-
-def near_kernel(blocks, top, *refs):
-    packed_refs, hidden_refs = refs[:blocks], refs[blocks : blocks + 2]
-    down_ref = refs[blocks + 2]
-    out_refs = refs[blocks + 3 : 2 * blocks + 3]
-    spread_ref, hidden_ref, total_ref = refs[2 * blocks + 3 :]
-    count = hidden_refs[0].shape[1]
+    )(*packed, *gates, *ups, in_hbm(w_gate), in_hbm(w_up), in_hbm(w_down))
+    return parts, down, near_hidden, own
+
+
+def near_kernel(blocks, pieces, top, *refs):
+    packed_refs, refs = refs[:blocks], refs[blocks:]
+    own_refs, refs = refs[:pieces], refs[pieces:]
+    beside_ref, down_ref, *refs = refs
+    out_refs = refs[:blocks]
+    spread_ref, hidden_ref, total_ref = refs[blocks:]
+    count = own_refs[0].shape[1]
     spread_shares(packed_refs, spread_ref, count, top, down_ref.shape[0])
-    hidden_ref[:, :count, :] = hidden_refs[0][...]
-    hidden_ref[:, count:, :] = hidden_refs[1][...]
+    begin = 0
+    for own_ref in own_refs:
+        end = begin + own_ref.shape[0]
+        hidden_ref[begin:end, :count, :] = own_ref[...]
+        begin = end
+    hidden_ref[:, count:, :] = beside_ref[...]
     project_into(
         out_refs, total_ref, spread_ref, down_ref, lambda member: hidden_ref[member], count
     )
 
 
-def near(packed, hiddens, down, kinds, top):
+def near(packed, owns, beside, down, kinds, top):
     blocks = len(packed)
-    local_experts, count, units = hiddens[0].shape
-    width = down.shape[2]
+    local_experts, units, width = down.shape
+    count = owns[0].shape[1]
     rows = blocks * count
     return pl.pallas_call(
-        functools.partial(near_kernel, blocks, top),
+        functools.partial(near_kernel, blocks, len(owns), top),
         out_shape=[jax.ShapeDtypeStruct((count, width), kind) for kind in kinds],
-        in_specs=[VMEM] * (blocks + 3),
+        in_specs=[VMEM] * (blocks + len(owns) + 2),
         out_specs=[VMEM] * blocks,
         scratch_shapes=[
             pltpu.VMEM((rows, slots_of(local_experts)), jnp.float32),
@@ -256,7 +308,7 @@
         cost_estimate=pl.CostEstimate(
             flops=2 * rows * down.size, bytes_accessed=2 * down.size, transcendentals=0
         ),
-    )(*packed, *hiddens, down)
+    )(*packed, *owns, beside, down)
 
 
 def exchange(array, pairs):
@@ -267,26 +319,35 @@
     peers = lax.axis_size("expert")
     count, top = expert_ids.shape
     packed = pack(tokens, expert_ids, route_scores)
-    if peers == 4:
-        pairs = {shift: [(i, i ^ shift) for i in range(peers)] for shift in (2, 3, 1)}
-        got = {s: exchange(packed, pairs[s]) for s in pairs}
-        gate, up, own = own_hidden(tokens, w_gate, w_up)
-        order = [got[3], got[2], got[1]]
-        parts, down, beside = far(order, 1, gate, up, w_down, count, top)
+    weights = (w_gate, w_up, w_down)
+    experts = w_gate.shape[0]
+    if peers == 4 and experts >= 4:
+        pairs = {shift: [(i, i ^ shift) for i in range(peers)] for shift in (2, 1)}
+        got = {shift: exchange(packed, pairs[shift]) for shift in pairs}
+        late = 1
+        cut = experts // 2
+        first = own_hidden(tokens, w_gate, w_up, 0, cut)
+        got[3] = exchange(got[2], pairs[1])
+        second = own_hidden(tokens, w_gate, w_up, cut, experts - late)
+        gates, ups, owns = zip(first, second)
+        order = [got[3], got[2], got[1], packed]
+        parts, down, beside, last = far(order, 1, gates, ups, weights, late, count, top)
         hop = exchange(parts[0], pairs[1])
         kinds = (jnp.float32, jnp.float32, jnp.bfloat16)
-        total, part, beside_part = near([packed, got[2], got[1]], [own, beside], down, kinds, top)
+        total, part, beside_part = near(
+            [packed, got[2], got[1]], [*owns, last], beside, down, kinds, top
+        )
         both = (part + hop.astype(jnp.float32)).astype(jnp.bfloat16)
         back = [exchange(both, pairs[2]), exchange(beside_part, pairs[1])]
         for part in back:
             total = total + part.astype(jnp.float32)
         return total.astype(jnp.bfloat16)
     got = lax.all_gather(packed, "expert")
-    gate, up, _ = own_hidden(tokens, w_gate, w_up)
+    gate, up, _ = own_hidden(tokens, w_gate, w_up, 0, experts)
     parts = []
     for start in range(0, peers, GROUP):
         here = [got[i] for i in range(start, min(start + GROUP, peers))]
-        parts += far(here, len(here), gate, up, w_down, count, top)[0]
+        parts += far(here, len(here), [gate], [up], weights, 0, count, top)[0]
     back = lax.all_to_all(jnp.stack(parts), "expert", 0, 0, tiled=True)
     return jnp.sum(back.astype(jnp.float32), axis=0).astype(jnp.bfloat16)
 

time: 39.1 us -> 45.5 us (1.16)
  starting transfers between devices: 9 us -> 11.9 us
  waiting for transfers between devices: 8.31 us -> 10.8 us
  Pallas kernels: 20.8 us -> 21.8 us
    ppermute x6, starting transfers between devices: 9 us -> 11.9 us  [exchange(): return lax.ppermute(array, 'expert', pairs)]
    ppermute x6, waiting for transfers between devices: 8.31 us -> 10.8 us  [exchange(): return lax.ppermute(array, 'expert', pairs)]
    pallas_call x3 -> x4, Pallas kernels: 19.8 us -> 20.9 us  [the longest x2 10.1 us: own_hidden(): pl.pallas_call(functools.partial(own_kernel, begin), out_shape=[pltpu.VME...]
  transfers between devices with their start and end apart: 6 -> 6, of which waited for: 4 -> 4; matrix products, arithmetic and copies ran while one was open for 0% -> 0% of each run, Pallas kernels for 31% -> 28%
where the time goes in v4:
time: 45.5 us; the launch traced here: 45.3 us
  Pallas kernels  21.8 us (48%)
  starting transfers between devices  11.9 us (26%)
  waiting for transfers between devices  10.8 us (24%)
  other arithmetic  0.73 us (2%)
    ppermute x6, starting transfers between devices, exchange(): return lax.ppermute(array, 'expert', pairs)  11.9 us
    ppermute x6, waiting for transfers between devices, exchange(): return lax.ppermute(array, 'expert', pairs)  10.8 us
    pallas_call x2, Pallas kernels, own_hidden(): pl.pallas_call(functools.partial(own_kernel, begin), out_shape=[pltpu.VME...  10.1 us
    pallas_call x1, Pallas kernels, far(): pl.pallas_call(functools.partial(far_kernel, blocks, sent, len(gates), la...  8.09 us
    pallas_call x1, Pallas kernels, near(): pl.pallas_call(functools.partial(near_kernel, blocks, len(owns), top), ou...  2.72 us
    pallas_call x1, Pallas kernels, pack(): pl.pallas_call(pack_kernel, out_shape=pltpu.VMEM((tiles.shape[0] + 2, SUB...  0.96 us
  transfers between devices with their start and end apart: 6, of which 4 were waited for; matrix products, arithmetic and copies ran while one was open for 0% of the time, Pallas kernels for 28%

profile of v4, /device:TPU:0, one launch (start us, length us, event | category | flops | bytes accessed | tf_op | source)
XLA Modules:
  0.0 45.3 jit_solution(17543650968071315351)
XLA Ops:
  0.0 1.0 %shard_map.64.refs_3_.refs_0_ = bf16[66,8,128]{2,1,0:T(8,128)(2,1)S(1)} custom-call(bf16[64,8,128]{2,1,0:T(8,128)(2,1)} %bitcast.7, s32[8,64]{1,0:T(8,128)} %bitcast.8, f32[8,64]{1,0:T(8,128)} %bitcast.9), custom_call_target="tpu_custom_call" | custom-call | tf_op jit(solution)/shard_map/pallas_call | solution.py:63
  1.0 4.1 %collective-permute-start = (bf16[66,8,128]{2,1,0:T(8,128)(2,1)S(1)}, bf16[66,8,128]{2,1,0:T(8,128)(2,1)S(1)}, u32[]{:S(2)}, u32[]{:S(2)}) collective-permute-start(bf16[66,8,128]{2,1,0:T(8,128)(2,1)S(1)} %shard_map.64.refs_3_.refs_0_), channel_id=1, source_target_pairs={{0,8},{4,12},{8,0},{12,4},{1,9},{5,13},{9,1},{13,5},{2,10},{6,14},... | collective-permute-start | bytes 405512 | tf_op jit(solution)/shard_map/ppermute | solution.py:315
  5.1 1.6 %collective-permute-start.1 = (bf16[66,8,128]{2,1,0:T(8,128)(2,1)S(1)}, bf16[66,8,128]{2,1,0:T(8,128)(2,1)S(1)}, u32[]{:S(2)}, u32[]{:S(2)}) collective-permute-start(bf16[66,8,128]{2,1,0:T(8,128)(2,1)S(1)} %shard_map.64.refs_3_.refs_0_), channel_id=1, source_target_pairs={{0,4},{4,0},{8,12},{12,8},{1,5},{5,1},{9,13},{13,9},{2,6},{6,2},{1... | collective-permute-start | bytes 405512 | tf_op jit(solution)/shard_map/ppermute | solution.py:315
  6.7 5.0 %collective-permute-done.refs_1_ = bf16[66,8,128]{2,1,0:T(8,128)(2,1)S(1)} collective-permute-done((bf16[66,8,128]{2,1,0:T(8,128)(2,1)S(1)}, bf16[66,8,128]{2,1,0:T(8,128)(2,1)S(1)}, u32[]{:S(2)}, u32[]{:S(2)}) %collective-permute-start) | collective-permute-done | bytes 135200 | tf_op jit(solution)/shard_map/ppermute | solution.py:315
  11.7 0.6 %collective-permute-start.2 = (bf16[66,8,128]{2,1,0:T(8,128)(2,1)S(1)}, bf16[66,8,128]{2,1,0:T(8,128)(2,1)S(1)}, u32[]{:S(2)}, u32[]{:S(2)}) collective-permute-start(bf16[66,8,128]{2,1,0:T(8,128)(2,1)S(1)} %collective-permute-done.refs_1_), channel_id=1, source_target_pairs={{0,4},{4,0},{8,12},{12,8},{1,5},{5,1},{9,13},{13,9},{2,6},{6,2},{1... | collective-permute-start | bytes 405512 | tf_op jit(solution)/shard_map/ppermute | solution.py:315
  12.3 4.6 %shard_map.66 = (bf16[3,1024,768]{2,1,0:T(8,128)(2,1)S(1)}, bf16[3,1024,768]{2,1,0:T(8,128)(2,1)S(1)}, bf16[3,64,768]{2,1,0:T(8,128)(2,1)S(1)}) custom-call(bf16[64,1024]{1,0:T(8,128)(2,1)} %token_hbm.3, bf16[8,1024,768]{2,1,0:T(8,128)(2,1)} %refs_8_.1, bf16[8,1024,768]{2,1,0:T(8,128)(2,1)} %refs_9_.1), custom_call_target="tpu_custom_call" | custom-call | flops 603979776 | bytes 9437184 | tf_op jit(solution)/shard_map/pallas_call | solution.py:106
  16.9 5.5 %shard_map.65 = (bf16[4,1024,768]{2,1,0:T(8,128)(2,1)S(1)}, bf16[4,1024,768]{2,1,0:T(8,128)(2,1)S(1)}, bf16[4,64,768]{2,1,0:T(8,128)(2,1)S(1)}) custom-call(bf16[64,1024]{1,0:T(8,128)(2,1)} %token_hbm.3, bf16[8,1024,768]{2,1,0:T(8,128)(2,1)} %refs_8_.1, bf16[8,1024,768]{2,1,0:T(8,128)(2,1)} %refs_9_.1), custom_call_target="tpu_custom_call" | custom-call | flops 805306368 | bytes 12582912 | tf_op jit(solution)/shard_map/pallas_call | solution.py:106
  22.4 0.0 collective-permute-done.1.refs_2_
  22.4 0.0 collective-permute-done.2.refs_0_
  22.4 8.1 %shard_map.67 = (bf16[64,1024]{1,0:T(8,128)(2,1)S(1)}, bf16[8,768,1024]{2,1,0:T(8,128)(2,1)S(1)}, bf16[8,128,768]{2,1,0:T(8,128)(2,1)S(1)}, bf16[1,64,768]{2,1,0:T(8,128)(2,1)S(1)}) custom-call(bf16[66,8,128]{2,1,0:T(8,128)(2,1)S(1)} %collective-permute-done.2.refs_0_, bf16[66,8,128]{2,1,0:T(8,128)(2,1)S(1)} %collective-permute-done.refs_1_, ...), custom_call_target="tpu_custom_call" | custom-call | flops 9663676416 | bytes 12582912 | tf_op jit(solution)/shard_map/pallas_call | solution.py:246
  30.5 1.5 %collective-permute-start.3 = (bf16[64,1024]{1,0:T(8,128)(2,1)S(1)}, bf16[64,1024]{1,0:T(8,128)(2,1)S(1)}, u32[]{:S(2)}, u32[]{:S(2)}) collective-permute-start(bf16[64,1024]{1,0:T(8,128)(2,1)S(1)} %get-tuple-element.29), channel_id=1, source_target_pairs={{0,4},{4,0},{8,12},{12,8},{1,5},{5,1},{9,13},{13,9},{2,6},{6,2},{1... | collective-permute-start | bytes 393224 | tf_op jit(solution)/shard_map/ppermute | solution.py:315
  32.0 2.7 %shard_map.68 = (f32[64,1024]{1,0:T(8,128)S(1)}, f32[64,1024]{1,0:T(8,128)S(1)}, bf16[64,1024]{1,0:T(8,128)(2,1)S(1)}) custom-call(bf16[66,8,128]{2,1,0:T(8,128)(2,1)S(1)} %shard_map.64.refs_3_.refs_0_, bf16[66,8,128]{2,1,0:T(8,128)(2,1)S(1)} %collective-permute-done.refs_1_, bf16[66,8,128]{2,1,0:T(8,128)(2,1)S(1)} %collective-permute-done.1.refs_2_, ...), custom_call_target="tpu_custom_call" | custom-call | flops 2415919104 | bytes 12582912 | tf_op jit(solution)/shard_map/pallas_call | solution.py:297
  34.7 0.7 %collective-permute-start.5 = (bf16[64,1024]{1,0:T(8,128)(2,1)S(1)}, bf16[64,1024]{1,0:T(8,128)(2,1)S(1)}, u32[]{:S(2)}, u32[]{:S(2)}) collective-permute-start(bf16[64,1024]{1,0:T(8,128)(2,1)S(1)} %get-tuple-element.30), channel_id=1, source_target_pairs={{0,4},{4,0},{8,12},{12,8},{1,5},{5,1},{9,13},{13,9},{2,6},{6,2},{1... | collective-permute-start | bytes 393224 | tf_op jit(solution)/shard_map/ppermute | solution.py:315
  35.4 0.3 collective-permute-done.3
  35.7 3.4 %collective-permute-start.4 = (bf16[64,1024]{1,0:T(8,128)(2,1)S(1)}, bf16[64,1024]{1,0:T(8,128)(2,1)S(1)}, u32[]{:S(2)}, u32[]{:S(2)}) collective-permute-start(bf16[64,1024]{1,0:T(8,128)(2,1)S(1)} %add_convert_fusion.1), channel_id=1, source_target_pairs={{0,8},{4,12},{8,0},{12,4},{1,9},{5,13},{9,1},{13,5},{2,10},{6,14},... | collective-permute-start | bytes 393224 | tf_op jit(solution)/shard_map/ppermute | solution.py:315
  39.2 2.3 %collective-permute-done.5 = bf16[64,1024]{1,0:T(8,128)(2,1)S(1)} collective-permute-done((bf16[64,1024]{1,0:T(8,128)(2,1)S(1)}, bf16[64,1024]{1,0:T(8,128)(2,1)S(1)}, u32[]{:S(2)}, u32[]{:S(2)}) %collective-permute-start.5) | collective-permute-done | bytes 131104 | tf_op jit(solution)/shard_map/ppermute | solution.py:315
  41.5 3.1 %collective-permute-done.4 = bf16[64,1024]{1,0:T(8,128)(2,1)S(1)} collective-permute-done((bf16[64,1024]{1,0:T(8,128)(2,1)S(1)}, bf16[64,1024]{1,0:T(8,128)(2,1)S(1)}, u32[]{:S(2)}, u32[]{:S(2)}) %collective-permute-start.4) | collective-permute-done | bytes 131104 | tf_op jit(solution)/shard_map/ppermute | solution.py:315
  44.6 0.7 %add_convert_fusion = bf16[64,1024]{1,0:T(8,128)(2,1)} fusion(bf16[64,1024]{1,0:T(8,128)(2,1)S(1)} %collective-permute-done.5, f32[64,1024]{1,0:T(8,128)S(1)} %get-tuple-element.27, bf16[64,1024]{1,0:T(8,128)(2,1)S(1)} %collective-permute-done.4), kind=kLoop, calls=%fused_computation | loop fusion | flops 327680 | bytes 655360 | tf_op jit(solution)/shard_map/convert_element_type | solution.py:344
  (1 shorter events, 0.0 us)
Async XLA Ops:
  1.0 10.7 %collective-permute-start = (bf16[66,8,128]{2,1,0:T(8,128)(2,1)S(1)}, bf16[66,8,128]{2,1,0:T(8,128)(2,1)S(1)}, u32[]{:S(2)}, u32[]{:S(2)}) collective-permute-start(bf16[66,8,128]{2,1,0:T(8,128)(2,1)S(1)} %shard_map.64.refs_3_.refs_0_), channel_id=1, source_target_pairs={{0,8},{4,12},{8,0},{12,4},{1,9},{5,13},{9,1},{13,5},{2,10},{6,14},... | collective-permute-start | bytes 405512 | tf_op jit(solution)/shard_map/ppermute | solution.py:315
  5.1 17.3 %collective-permute-start.1 = (bf16[66,8,128]{2,1,0:T(8,128)(2,1)S(1)}, bf16[66,8,128]{2,1,0:T(8,128)(2,1)S(1)}, u32[]{:S(2)}, u32[]{:S(2)}) collective-permute-start(bf16[66,8,128]{2,1,0:T(8,128)(2,1)S(1)} %shard_map.64.refs_3_.refs_0_), channel_id=1, source_target_pairs={{0,4},{4,0},{8,12},{12,8},{1,5},{5,1},{9,13},{13,9},{2,6},{6,2},{1... | collective-permute-start | bytes 405512 | tf_op jit(solution)/shard_map/ppermute | solution.py:315
  11.7 10.7 %collective-permute-start.2 = (bf16[66,8,128]{2,1,0:T(8,128)(2,1)S(1)}, bf16[66,8,128]{2,1,0:T(8,128)(2,1)S(1)}, u32[]{:S(2)}, u32[]{:S(2)}) collective-permute-start(bf16[66,8,128]{2,1,0:T(8,128)(2,1)S(1)} %collective-permute-done.refs_1_), channel_id=1, source_target_pairs={{0,4},{4,0},{8,12},{12,8},{1,5},{5,1},{9,13},{13,9},{2,6},{6,2},{1... | collective-permute-start | bytes 405512 | tf_op jit(solution)/shard_map/ppermute | solution.py:315
  30.5 5.2 %collective-permute-start.3 = (bf16[64,1024]{1,0:T(8,128)(2,1)S(1)}, bf16[64,1024]{1,0:T(8,128)(2,1)S(1)}, u32[]{:S(2)}, u32[]{:S(2)}) collective-permute-start(bf16[64,1024]{1,0:T(8,128)(2,1)S(1)} %get-tuple-element.29), channel_id=1, source_target_pairs={{0,4},{4,0},{8,12},{12,8},{1,5},{5,1},{9,13},{13,9},{2,6},{6,2},{1... | collective-permute-start | bytes 393224 | tf_op jit(solution)/shard_map/ppermute | solution.py:315
  34.7 6.8 %collective-permute-start.5 = (bf16[64,1024]{1,0:T(8,128)(2,1)S(1)}, bf16[64,1024]{1,0:T(8,128)(2,1)S(1)}, u32[]{:S(2)}, u32[]{:S(2)}) collective-permute-start(bf16[64,1024]{1,0:T(8,128)(2,1)S(1)} %get-tuple-element.30), channel_id=1, source_target_pairs={{0,4},{4,0},{8,12},{12,8},{1,5},{5,1},{9,13},{13,9},{2,6},{6,2},{1... | collective-permute-start | bytes 393224 | tf_op jit(solution)/shard_map/ppermute | solution.py:315
  35.7 8.9 %collective-permute-start.4 = (bf16[64,1024]{1,0:T(8,128)(2,1)S(1)}, bf16[64,1024]{1,0:T(8,128)(2,1)S(1)}, u32[]{:S(2)}, u32[]{:S(2)}) collective-permute-start(bf16[64,1024]{1,0:T(8,128)(2,1)S(1)} %add_convert_fusion.1), channel_id=1, source_target_pairs={{0,8},{4,12},{8,0},{12,4},{1,9},{5,13},{9,1},{13,5},{2,10},{6,14},... | collective-permute-start | bytes 393224 | tf_op jit(solution)/shard_map/ppermute | solution.py:315

commit v5 on v3

--- a/solution.py
+++ b/solution.py
@@ -10,6 +10,7 @@
 
 SUBLANES, LANES = 8, 128
 CHUNK = 256
+PIECES = 4
 GROUP = 4
 MIB = 1 << 20
 VMEM = pl.BlockSpec(memory_space=pltpu.VMEM)
@@ -41,8 +42,13 @@
     copies = [
         pltpu.make_async_copy(id_hbm, id_ref, sems.at[0]),
         pltpu.make_async_copy(score_hbm, score_ref, sems.at[1]),
-        pltpu.make_async_copy(tile_hbm, out_ref.at[pl.ds(0, tiles)], sems.at[2]),
     ]
+    piece = -(-tiles // PIECES)
+    for index, begin in enumerate(range(0, tiles, piece)):
+        span = pl.ds(begin, min(piece, tiles - begin))
+        copies.append(
+            pltpu.make_async_copy(tile_hbm.at[span], out_ref.at[span], sems.at[2 + index])
+        )
     for copy in copies:
         copy.start()
     out_ref[tiles] = jnp.zeros((SUBLANES, LANES), jnp.bfloat16)
@@ -54,7 +60,8 @@
     shares = scores / jnp.sum(scores, axis=0, keepdims=True)
     out_ref[tiles, :top, :count] = id_ref[...].astype(jnp.float32).astype(jnp.bfloat16)
     out_ref[tiles + 1, :top, :count] = shares.astype(jnp.bfloat16)
-    copies[2].wait()
+    for copy in copies[2:]:
+        copy.wait()
 
 
 def pack(tokens, expert_ids, route_scores):
@@ -68,7 +75,7 @@
         scratch_shapes=[
             pltpu.VMEM((top, count), jnp.int32),
             pltpu.VMEM((top, count), jnp.float32),
-            pltpu.SemaphoreType.DMA((3,)),
+            pltpu.SemaphoreType.DMA((2 + PIECES,)),
         ],
         compiler_params=pltpu.CompilerParams(vmem_limit_bytes=4 * MIB),
     )(in_hbm(tiles), in_hbm(expert_ids.T), in_hbm(route_scores.T))

time: 39.1 us -> 39 us (level)
  no operation moved by 1% of the time
where the time goes in v5:
time: 39 us; the launch traced here: 38.8 us
  Pallas kernels  20.7 us (53%)
  starting transfers between devices  9.01 us (23%)
  waiting for transfers between devices  8.32 us (21%)
  other arithmetic  0.73 us (2%)
    pallas_call x1, Pallas kernels, own_hidden(): pl.pallas_call(own_kernel, out_shape=[pltpu.VMEM(w_gate.shape, w_gate.dty...  9.15 us
    ppermute x6, starting transfers between devices, exchange(): return lax.ppermute(array, 'expert', pairs)  9.01 us
    ppermute x6, waiting for transfers between devices, exchange(): return lax.ppermute(array, 'expert', pairs)  8.32 us
    pallas_call x1, Pallas kernels, far(): pl.pallas_call(functools.partial(far_kernel, blocks, sent, top), out_shap...  7.84 us
    pallas_call x1, Pallas kernels, near(): pl.pallas_call(functools.partial(near_kernel, blocks, top), out_shape=[ja...  2.8 us
    pallas_call x1, Pallas kernels, pack(): pl.pallas_call(pack_kernel, out_shape=pltpu.VMEM((tiles.shape[0] + 2, SUB...  0.89 us
  transfers between devices with their start and end apart: 6, of which 4 were waited for; matrix products, arithmetic and copies ran while one was open for 0% of the time, Pallas kernels for 31%

profile of v5, /device:TPU:0, one launch (start us, length us, event | category | flops | bytes accessed | tf_op | source)
XLA Modules:
  0.0 38.8 jit_solution(2393740996234013273)
XLA Ops:
  0.0 0.9 %shard_map.64.refs_0_ = bf16[66,8,128]{2,1,0:T(8,128)(2,1)S(1)} custom-call(bf16[64,8,128]{2,1,0:T(8,128)(2,1)} %bitcast.7, s32[8,64]{1,0:T(8,128)} %bitcast.8, f32[8,64]{1,0:T(8,128)} %bitcast.9), custom_call_target="tpu_custom_call" | custom-call | tf_op jit(solution)/shard_map/pallas_call | solution.py:70
  0.9 5.1 %collective-permute-start.2 = (bf16[66,8,128]{2,1,0:T(8,128)(2,1)S(1)}, bf16[66,8,128]{2,1,0:T(8,128)(2,1)S(1)}, u32[]{:S(2)}, u32[]{:S(2)}) collective-permute-start(bf16[66,8,128]{2,1,0:T(8,128)(2,1)S(1)} %shard_map.64.refs_0_), channel_id=1, source_target_pairs={{0,12},{4,8},{8,4},{12,0},{1,13},{5,9},{9,5},{13,1},{2,14},{6,10},... | collective-permute-start | bytes 405512 | tf_op jit(solution)/shard_map/ppermute | solution.py:270
  6.0 0.0 collective-permute-start.1
  6.0 0.6 %collective-permute-start = (bf16[66,8,128]{2,1,0:T(8,128)(2,1)S(1)}, bf16[66,8,128]{2,1,0:T(8,128)(2,1)S(1)}, u32[]{:S(2)}, u32[]{:S(2)}) collective-permute-start(bf16[66,8,128]{2,1,0:T(8,128)(2,1)S(1)} %shard_map.64.refs_0_), channel_id=1, source_target_pairs={{0,8},{4,12},{8,0},{12,4},{1,9},{5,13},{9,1},{13,5},{2,10},{6,14},... | collective-permute-start | bytes 405512 | tf_op jit(solution)/shard_map/ppermute | solution.py:270
  6.7 9.2 %shard_map.65 = (bf16[8,1024,768]{2,1,0:T(8,128)(2,1)S(1)}, bf16[8,1024,768]{2,1,0:T(8,128)(2,1)S(1)}, bf16[8,64,768]{2,1,0:T(8,128)(2,1)S(1)}) custom-call(bf16[64,1024]{1,0:T(8,128)(2,1)} %token_hbm.1, bf16[8,1024,768]{2,1,0:T(8,128)(2,1)} %gate_hbm.1, bf16[8,1024,768]{2,1,0:T(8,128)(2,1)} %up_hbm.1), custom_call_target="tpu_custom_call" | custom-call | flops 1610612736 | bytes 25165824 | tf_op jit(solution)/shard_map/pallas_call | solution.py:112
  15.8 0.0 collective-permute-done.2.refs_0_
  15.9 0.0 collective-permute-done.1.refs_2_
  15.9 1.6 %collective-permute-done.refs_1_ = bf16[66,8,128]{2,1,0:T(8,128)(2,1)S(1)} collective-permute-done((bf16[66,8,128]{2,1,0:T(8,128)(2,1)S(1)}, bf16[66,8,128]{2,1,0:T(8,128)(2,1)S(1)}, u32[]{:S(2)}, u32[]{:S(2)}) %collective-permute-start) | collective-permute-done | bytes 135200 | tf_op jit(solution)/shard_map/ppermute | solution.py:270
  17.5 7.8 %shard_map.66 = (bf16[64,1024]{1,0:T(8,128)(2,1)S(1)}, bf16[8,768,1024]{2,1,0:T(8,128)(2,1)S(1)}, bf16[8,128,768]{2,1,0:T(8,128)(2,1)S(1)}) custom-call(bf16[66,8,128]{2,1,0:T(8,128)(2,1)S(1)} %collective-permute-done.2.refs_0_, bf16[66,8,128]{2,1,0:T(8,128)(2,1)S(1)} %collective-permute-done.refs_1_, ...), custom_call_target="tpu_custom_call" | custom-call | flops 7247757312 | bytes 12582912 | tf_op jit(solution)/shard_map/pallas_call | solution.py:209
  25.3 0.1 collective-permute-start.3
  25.4 2.8 %shard_map.67 = (f32[64,1024]{1,0:T(8,128)S(1)}, f32[64,1024]{1,0:T(8,128)S(1)}, bf16[64,1024]{1,0:T(8,128)(2,1)S(1)}) custom-call(bf16[66,8,128]{2,1,0:T(8,128)(2,1)S(1)} %shard_map.64.refs_0_, bf16[66,8,128]{2,1,0:T(8,128)(2,1)S(1)} %collective-permute-done.refs_1_, bf16[66,8,128]{2,1,0:T(8,128)(2,1)S(1)} %collective-permute-done.1.refs_2_, ...), custom_call_target="tpu_custom_call" | custom-call | flops 2415919104 | bytes 12582912 | tf_op jit(solution)/shard_map/pallas_call | solution.py:252
  28.2 2.1 %collective-permute-start.5 = (bf16[64,1024]{1,0:T(8,128)(2,1)S(1)}, bf16[64,1024]{1,0:T(8,128)(2,1)S(1)}, u32[]{:S(2)}, u32[]{:S(2)}) collective-permute-start(bf16[64,1024]{1,0:T(8,128)(2,1)S(1)} %get-tuple-element.22), channel_id=1, source_target_pairs={{0,4},{4,0},{8,12},{12,8},{1,5},{5,1},{9,13},{13,9},{2,6},{6,2},{1... | collective-permute-start | bytes 393224 | tf_op jit(solution)/shard_map/ppermute | solution.py:270
  30.3 0.4 collective-permute-done.3
  30.7 1.1 %collective-permute-start.4 = (bf16[64,1024]{1,0:T(8,128)(2,1)S(1)}, bf16[64,1024]{1,0:T(8,128)(2,1)S(1)}, u32[]{:S(2)}, u32[]{:S(2)}) collective-permute-start(bf16[64,1024]{1,0:T(8,128)(2,1)S(1)} %add_convert_fusion.1), channel_id=1, source_target_pairs={{0,8},{4,12},{8,0},{12,4},{1,9},{5,13},{9,1},{13,5},{2,10},{6,14},... | collective-permute-start | bytes 393224 | tf_op jit(solution)/shard_map/ppermute | solution.py:270
  31.8 2.3 %collective-permute-done.5 = bf16[64,1024]{1,0:T(8,128)(2,1)S(1)} collective-permute-done((bf16[64,1024]{1,0:T(8,128)(2,1)S(1)}, bf16[64,1024]{1,0:T(8,128)(2,1)S(1)}, u32[]{:S(2)}, u32[]{:S(2)}) %collective-permute-start.5) | collective-permute-done | bytes 131104 | tf_op jit(solution)/shard_map/ppermute | solution.py:270
  34.0 4.1 %collective-permute-done.4 = bf16[64,1024]{1,0:T(8,128)(2,1)S(1)} collective-permute-done((bf16[64,1024]{1,0:T(8,128)(2,1)S(1)}, bf16[64,1024]{1,0:T(8,128)(2,1)S(1)}, u32[]{:S(2)}, u32[]{:S(2)}) %collective-permute-start.4) | collective-permute-done | bytes 131104 | tf_op jit(solution)/shard_map/ppermute | solution.py:270
  38.1 0.7 %add_convert_fusion = bf16[64,1024]{1,0:T(8,128)(2,1)} fusion(bf16[64,1024]{1,0:T(8,128)(2,1)S(1)} %collective-permute-done.5, f32[64,1024]{1,0:T(8,128)S(1)} %get-tuple-element.19, bf16[64,1024]{1,0:T(8,128)(2,1)S(1)} %collective-permute-done.4), kind=kLoop, calls=%fused_computation | loop fusion | flops 327680 | bytes 655360 | tf_op jit(solution)/shard_map/convert_element_type | solution.py:290
  (1 shorter events, 0.0 us)
Async XLA Ops:
  0.9 14.9 %collective-permute-start.2 = (bf16[66,8,128]{2,1,0:T(8,128)(2,1)S(1)}, bf16[66,8,128]{2,1,0:T(8,128)(2,1)S(1)}, u32[]{:S(2)}, u32[]{:S(2)}) collective-permute-start(bf16[66,8,128]{2,1,0:T(8,128)(2,1)S(1)} %shard_map.64.refs_0_), channel_id=1, source_target_pairs={{0,12},{4,8},{8,4},{12,0},{1,13},{5,9},{9,5},{13,1},{2,14},{6,10},... | collective-permute-start | bytes 405512 | tf_op jit(solution)/shard_map/ppermute | solution.py:270
  6.0 9.8 %collective-permute-start.1 = (bf16[66,8,128]{2,1,0:T(8,128)(2,1)S(1)}, bf16[66,8,128]{2,1,0:T(8,128)(2,1)S(1)}, u32[]{:S(2)}, u32[]{:S(2)}) collective-permute-start(bf16[66,8,128]{2,1,0:T(8,128)(2,1)S(1)} %shard_map.64.refs_0_), channel_id=1, source_target_pairs={{0,4},{4,0},{8,12},{12,8},{1,5},{5,1},{9,13},{13,9},{2,6},{6,2},{1... | collective-permute-start | bytes 405512 | tf_op jit(solution)/shard_map/ppermute | solution.py:270
  6.0 11.4 %collective-permute-start = (bf16[66,8,128]{2,1,0:T(8,128)(2,1)S(1)}, bf16[66,8,128]{2,1,0:T(8,128)(2,1)S(1)}, u32[]{:S(2)}, u32[]{:S(2)}) collective-permute-start(bf16[66,8,128]{2,1,0:T(8,128)(2,1)S(1)} %shard_map.64.refs_0_), channel_id=1, source_target_pairs={{0,8},{4,12},{8,0},{12,4},{1,9},{5,13},{9,1},{13,5},{2,10},{6,14},... | collective-permute-start | bytes 405512 | tf_op jit(solution)/shard_map/ppermute | solution.py:270
  25.3 5.3 %collective-permute-start.3 = (bf16[64,1024]{1,0:T(8,128)(2,1)S(1)}, bf16[64,1024]{1,0:T(8,128)(2,1)S(1)}, u32[]{:S(2)}, u32[]{:S(2)}) collective-permute-start(bf16[64,1024]{1,0:T(8,128)(2,1)S(1)} %get-tuple-element.21), channel_id=1, source_target_pairs={{0,4},{4,0},{8,12},{12,8},{1,5},{5,1},{9,13},{13,9},{2,6},{6,2},{1... | collective-permute-start | bytes 393224 | tf_op jit(solution)/shard_map/ppermute | solution.py:270
  28.2 5.8 %collective-permute-start.5 = (bf16[64,1024]{1,0:T(8,128)(2,1)S(1)}, bf16[64,1024]{1,0:T(8,128)(2,1)S(1)}, u32[]{:S(2)}, u32[]{:S(2)}) collective-permute-start(bf16[64,1024]{1,0:T(8,128)(2,1)S(1)} %get-tuple-element.22), channel_id=1, source_target_pairs={{0,4},{4,0},{8,12},{12,8},{1,5},{5,1},{9,13},{13,9},{2,6},{6,2},{1... | collective-permute-start | bytes 393224 | tf_op jit(solution)/shard_map/ppermute | solution.py:270
  30.7 7.4 %collective-permute-start.4 = (bf16[64,1024]{1,0:T(8,128)(2,1)S(1)}, bf16[64,1024]{1,0:T(8,128)(2,1)S(1)}, u32[]{:S(2)}, u32[]{:S(2)}) collective-permute-start(bf16[64,1024]{1,0:T(8,128)(2,1)S(1)} %add_convert_fusion.1), channel_id=1, source_target_pairs={{0,8},{4,12},{8,0},{12,4},{1,9},{5,13},{9,1},{13,5},{2,10},{6,14},... | collective-permute-start | bytes 393224 | tf_op jit(solution)/shard_map/ppermute | solution.py:270
